TPU v7x, 256 devices: a whole 4x4x8 slice. The times are simulated.
256 devices in a mesh: row: 16 (over z, y_hi), col: 16 (over x, y_lo, core).
Axes of the slice: x: 4, y: 4 (y_hi: 2, y_lo: 2; y = y_hi * 2 + y_lo), z: 8, core: 2. Of those that a mesh axis runs over, the one named last changes fastest.
Arguments:
- patches: bfloat16 [32, 8, 8, 8192], P('row', None, None, 'col'), may hold values from -6 to 6
- out_grad: bfloat16 [32, 8, 8, 8192], P('row', None, None, 'col'), may hold values from -6 to 6
- conv_kernel: float32 [3, 3, 3, 8192], P(None, None, None, 'col'), may hold values from -1.25 to 1.25
- saved_gate: bfloat16 [2048, 14336], P('col', 'row'), may hold values from -6 to 6
- saved_up: bfloat16 [2048, 14336], P('col', 'row'), may hold values from -6 to 6
- w_gate: bfloat16 [8192, 14336], P('col', 'row'), may hold values from -0.0625 to 0.0625
- w_up: bfloat16 [8192, 14336], P('col', 'row'), may hold values from -0.0625 to 0.0625
- w_down: bfloat16 [14336, 8192], P('row', 'col'), may hold values from -0.046875 to 0.046875
Outputs:
- patch_grad: bfloat16 [32, 8, 8, 8192], P('row', None, None, 'col')
- kernel_grad: float32 [3, 3, 3, 8192], P(None, None, None, 'col')
- gate_wgrad: bfloat16 [8192, 14336], P('col', 'row')
- up_wgrad: bfloat16 [8192, 14336], P('col', 'row')
- down_wgrad: bfloat16 [14336, 8192], P('row', 'col')
All inputs are finite; a program needn't handle non-finite values.
Results may differ from a plain program's by a relative error of at most 0.02.
Values may be sent and summed in bfloat16 or wider, within the bound.
A program may use at most 128 MiB of HBM per device.

v0:
```python
import jax
import jax.numpy as jnp
from jax import lax
from jax.sharding import PartitionSpec as P


def padded(x, sides, width):
    for axis, dim in sides:
        peers, length = (lax.axis_size(axis), x.shape[dim])
        up = [(i, (i + 1) % peers) for i in range(peers - 1)]
        down = [(j, i) for i, j in up]
        last = lax.slice_in_dim(x, length - width, length, axis=dim)
        first = lax.slice_in_dim(x, 0, width, axis=dim)
        before = lax.ppermute(last, axis, up)
        after = lax.ppermute(first, axis, down)
        x = jnp.concatenate([before, x, after], axis=dim)
    return x


def in_one_piece(arrays, axis, dim, along):
    ends, at = ([], 0)
    for a in arrays[:-1]:
        at += a.shape[along]
        ends.append(at)
    both = jnp.concatenate(arrays, axis=along)
    return tuple(jnp.split(lax.all_gather(both, axis, axis=dim, tiled=True), ends, axis=along))


def in_blocks(x, dim, peers):
    dims = x.shape
    blocks = x.reshape(*dims[:dim], peers, dims[dim] // peers, *dims[dim + 1 :])
    return jnp.moveaxis(blocks, dim, 0)


def sum_at_owner(x, axis, dim):
    peers = lax.axis_size(axis)
    blocks = lax.all_to_all(in_blocks(x, dim, peers), axis, 0, 0, tiled=True)
    return jnp.sum(blocks.astype(jnp.float32), axis=0)


def from_everyone(x, axis):
    peers = lax.axis_size(axis)
    return lax.all_to_all(jnp.broadcast_to(x[None], (peers, *x.shape)), axis, 0, 0, tiled=True)


def of_everyone(x, axis):
    everything = from_everyone(x, axis)
    return jnp.sum(everything.astype(jnp.float32), axis=0)


def correlate(framed, kernel, flipped):
    planes = framed.shape[0] - 2
    height = framed.shape[1] - 2
    breadth = framed.shape[2] - 2
    summed = jnp.zeros((planes, height, breadth, framed.shape[3]), jnp.float32)
    for along_z in range(3):
        for along_y in range(3):
            for along_x in range(3):
                if flipped:
                    lead_z, lead_y, lead_x = (2 - along_z, 2 - along_y, 2 - along_x)
                else:
                    lead_z, lead_y, lead_x = (along_z, along_y, along_x)
                window = framed[
                    lead_z : lead_z + planes, lead_y : lead_y + height, lead_x : lead_x + breadth
                ]
                summed = summed + kernel[along_z, along_y, along_x] * window
    return summed


def frame_sides(field):
    return jnp.pad(field, ((0, 0), (1, 1), (1, 1), (0, 0)))


def tap_sums(grads, framed):
    planes, height, breadth = (grads.shape[0], grads.shape[1], grads.shape[2])
    layers = []
    for along_z in range(3):
        for along_y in range(3):
            for along_x in range(3):
                window = framed[
                    along_z : along_z + planes,
                    along_y : along_y + height,
                    along_x : along_x + breadth,
                ]
                layers.append(jnp.sum(grads * window, axis=(0, 1, 2)))
    return jnp.stack(layers).reshape(3, 3, 3, grads.shape[3])


def swiglu_back(hidden_grad, gate_in, up_in):
    gate_f = gate_in.astype(jnp.float32)
    up_f = up_in.astype(jnp.float32)
    sigmoid_g = jax.nn.sigmoid(gate_f)
    silu_g = gate_f * sigmoid_g
    hidden_act = (silu_g * up_f).astype(jnp.bfloat16)
    gate_grad = (hidden_grad * up_f * sigmoid_g * (1.0 + gate_f * (1.0 - sigmoid_g))).astype(
        jnp.bfloat16
    )
    up_grad = (hidden_grad * silu_g).astype(jnp.bfloat16)
    return (hidden_act, gate_grad, up_grad)


def body(patches, out_grad, conv_kernel, saved_gate, saved_up, w_gate, w_up, w_down):
    planes, height, breadth, features = patches.shape
    rimmed = padded(patches, (("row", 0),), 1)
    framed_in = frame_sides(rimmed.astype(jnp.float32))
    mixed_in = (patches.astype(jnp.float32) + correlate(framed_in, conv_kernel, False)).astype(
        jnp.bfloat16
    )
    whole_in, whole_grad = in_one_piece((mixed_in, out_grad), "row", 0, 1)
    all_rows = whole_in.shape[0] * height * breadth
    flat_in = whole_in.reshape(all_rows, features)
    flat_grad = whole_grad.reshape(all_rows, features)
    contract_cols = (((1,), (1,)), ((), ()))
    contract_rows = (((0,), (0,)), ((), ()))
    partial_value = lax.dot_general(
        flat_grad, w_down, contract_cols, preferred_element_type=jnp.float32
    )
    hidden_grad = sum_at_owner(partial_value.astype(jnp.bfloat16), "col", 0)
    hidden_act, gate_grad, up_grad = swiglu_back(hidden_grad, saved_gate, saved_up)
    hidden_all, gate_grad_all, up_grad_all = in_one_piece(
        (hidden_act, gate_grad, up_grad), "col", 0, 1
    )
    down_wgrad = lax.dot_general(
        hidden_all, flat_grad, contract_rows, preferred_element_type=jnp.float32
    ).astype(jnp.bfloat16)
    gate_wgrad = lax.dot_general(
        flat_in, gate_grad_all, contract_rows, preferred_element_type=jnp.float32
    ).astype(jnp.bfloat16)
    up_wgrad = lax.dot_general(
        flat_in, up_grad_all, contract_rows, preferred_element_type=jnp.float32
    ).astype(jnp.bfloat16)
    term = lax.dot_general(gate_grad_all, w_gate, contract_cols, preferred_element_type=jnp.float32)
    mlp_grad = sum_at_owner(
        (
            term
            + lax.dot_general(up_grad_all, w_up, contract_cols, preferred_element_type=jnp.float32)
        ).astype(jnp.bfloat16),
        "row",
        0,
    )
    total_grad = out_grad.astype(jnp.float32) + mlp_grad.reshape(planes, height, breadth, features)
    grad_rimmed = padded(total_grad.astype(jnp.bfloat16), (("row", 0),), 1).astype(total_grad.dtype)
    patch_grad = (total_grad + correlate(frame_sides(grad_rimmed), conv_kernel, True)).astype(
        jnp.bfloat16
    )
    kernel_grad = of_everyone(tap_sums(total_grad, framed_in).astype(jnp.bfloat16), "row").astype(
        jnp.float32
    )
    return (patch_grad, kernel_grad, gate_wgrad, up_wgrad, down_wgrad)


def solution(mesh):
    return jax.shard_map(
        body,
        mesh=mesh,
        in_specs=(
            P("row", None, None, "col"),
            P("row", None, None, "col"),
            P(None, None, None, "col"),
            P("col", "row"),
            P("col", "row"),
            P("col", "row"),
            P("col", "row"),
            P("row", "col"),
        ),
        out_specs=(
            P("row", None, None, "col"),
            P(None, None, None, "col"),
            P("col", "row"),
            P("col", "row"),
            P("row", "col"),
        ),
        check_vma=False,
    )
```

profile of v0, /device:TPU:2, one launch (start us, length us, event | category | flops | bytes accessed | tf_op | source)
XLA Modules:
  0.0 361.6 jit_solution(22198173800170470)
XLA Ops:
  7.2 0.0 copy-start
  7.2 0.0 copy-start.3
  7.2 0.0 all-gather.3.cloned.1.call-start
  7.2 1.0 fusion.83
  8.2 5.1 %collective-permute-start = (bf16[1,8,8,512]{3,2,1,0:T(8,128)(2,1)S(1)}, bf16[1,8,8,512]{3,2,1,0:T(8,128)(2,1)S(1)}, u32[]{:S(2)}, u32[]{:S(2)}) collective-permute-start(bf16[1,8,8,512]{3,2,1,0:T(8,128)(2,1)S(1)} %get-tuple-element.41), channel_id=1, source_target_pairs={{0,16},{16,32},{32,48},{48,64},{64,80},{80,96},{96,112},{112,128},... | collective-permute-start | bytes 196616 | tf_op jit(solution)/shard_map/ppermute | solution.py:14
  13.3 1.3 collective-permute-start.1
  14.6 0.9 fusion.84
  15.7 0.8 fusion.85
  16.6 0.0 copy-start.49
  16.6 0.0 copy-start.51
  16.6 4.4 %collective-permute-done.1 = bf16[1,8,8,512]{3,2,1,0:T(8,128)(2,1)S(1)} collective-permute-done((bf16[1,8,8,512]{3,2,1,0:T(8,128)(2,1)S(1)}, bf16[1,8,8,512]{3,2,1,0:T(8,128)(2,1)S(1)}, u32[]{:S(2)}, u32[]{:S(2)}) %collective-permute-start.1) | collective-permute-done | bytes 65568 | tf_op jit(solution)/shard_map/ppermute | solution.py:15
  21.0 0.9 maximum_convert_fusion
  21.9 1.5 add_convert_fusion.1
  23.5 0.7 pad_maximum_fusion.1
  24.2 0.0 all-gather.3.cloned.1.call-update
  24.2 0.0 all-gather.5.cloned.1.call-start
  24.3 103.0 %all-gather.3.cloned.1.call-done = bf16[32,16,8,512]{3,2,1,0:T(8,128)(2,1)} async-done(((bf16[2,16,8,512]{3,2,1,0:T(8,128)(2,1)}), bf16[32,16,8,512]{3,2,1,0:T(8,128)(2,1)}) %all-gather.3.cloned.1.call-update) | async-done | bytes 4194320 | tf_op jit(solution)/shard_map/all_gather | solution.py:26
  127.3 3.9 %fusion.81 = (bf16[32,8,8,512]{3,2,1,0:T(8,128)(2,1)}, bf16[32,8,8,512]{3,2,1,0:T(8,128)(2,1)S(1)}) fusion(bf16[32,16,8,512]{3,2,1,0:T(8,128)(2,1)} %all-gather.3.cloned.1.call-done), kind=kLoop, calls=%fused_computation.168 | loop fusion | bytes 8388608 | tf_op jit(solution)/shard_map/split | solution.py:26
  131.4 2.4 convolution_convert_fusion
  133.9 46.9 %all_to_all.15 = bf16[16,128,896]{2,1,0:T(8,128)(2,1)S(1)} all-to-all(bf16[16,128,896]{2,1,0:T(8,128)(2,1)S(1)} %bitcast.40), channel_id=1, replica_groups=mesh['row'=16,'col'=16] {'col'}, dimensions={0} | all-to-all | bytes 7340032 | tf_op jit(solution)/shard_map/all_to_all | solution.py:37
  180.7 0.5 convert_reduce_fusion
  181.2 0.4 copy-done.5
  181.6 0.1 copy-done.6
  181.8 0.3 fusion.24
  182.1 0.9 pad_maximum_fusion
  183.0 0.0 all-gather.5.cloned.1.call-update
  183.0 64.2 %all-gather.5.cloned.1.call-done = bf16[2048,2688]{1,0:T(8,128)(2,1)} async-done(((bf16[128,2688]{1,0:T(8,128)(2,1)}), bf16[2048,2688]{1,0:T(8,128)(2,1)}) %all-gather.5.cloned.1.call-update) | async-done | bytes 11010064 | tf_op jit(solution)/shard_map/all_gather | solution.py:26
  247.2 4.6 %fusion.4 = f32[2048,512]{1,0:T(8,128)S(1)} fusion(bf16[512,896]{1,0:T(8,128)(2,1)S(1)} %copy-done.54, bf16[2048,2688]{1,0:T(8,128)(2,1)} %all-gather.5.cloned.1.call-done), kind=kOutput, calls=%fused_computation.56 | convolution fusion | flops 1879048192 | bytes 8781824 | tf_op jit(solution)/shard_map/dot_general | solution.py:136
  251.9 0.6 copy-done.53
  252.5 3.8 %add_convert_fusion = bf16[2048,512]{1,0:T(8,128)(2,1)} fusion(f32[2048,512]{1,0:T(8,128)S(1)} %fusion.4, bf16[512,896]{1,0:T(8,128)(2,1)S(1)} %copy-done.55, bf16[2048,2688]{1,0:T(8,128)(2,1)S(1)} %copy-done.53), kind=kOutput, calls=%fused_computation.50 | convolution fusion | flops 1881145344 | bytes 10878976 | tf_op jit(solution)/shard_map/dot_general | solution.py:132
  256.3 9.6 %all-to-all-start.1 = ((bf16[16,128,512]{2,1,0:T(8,128)(2,1)}), bf16[16,128,512]{2,1,0:T(8,128)(2,1)S(1)}, u32[]{:S(2)}, u32[]{:S(2)}) async-start(bf16[16,128,512]{2,1,0:T(8,128)(2,1)} %bitcast.41), calls=%async_computation.1 | async-start | bytes 4194304 | tf_op jit(solution)/shard_map/all_to_all | solution.py:37
  265.9 6.1 %fusion.12 = bf16[512,896]{1,0:T(8,128)(2,1)} fusion(bf16[2048,512]{1,0:T(8,128)(2,1)} %bitcast.42, bf16[2048,2688]{1,0:T(8,128)(2,1)} %all-gather.5.cloned.1.call-done), kind=kOutput, calls=%fused_computation.62 | convolution fusion | flops 1879506944 | bytes 6684672 | tf_op jit(solution)/shard_map/dot_general | solution.py:126
  272.0 5.1 %fusion.18 = bf16[896,512]{1,0:T(8,128)(2,1)} fusion(bf16[2048,512]{1,0:T(8,128)(2,1)S(1)} %bitcast.45, bf16[2048,2688]{1,0:T(8,128)(2,1)} %all-gather.5.cloned.1.call-done), kind=kOutput, calls=%fused_computation.64 | convolution fusion | flops 1879506944 | bytes 6684672 | tf_op jit(solution)/shard_map/dot_general | solution.py:123
  277.1 41.0 %all-to-all-done.1 = bf16[16,128,512]{2,1,0:T(8,128)(2,1)S(1)} async-done(((bf16[16,128,512]{2,1,0:T(8,128)(2,1)}), bf16[16,128,512]{2,1,0:T(8,128)(2,1)S(1)}, u32[]{:S(2)}, u32[]{:S(2)}) %all-to-all-start.1) | async-done | bytes 2097184 | tf_op jit(solution)/shard_map/all_to_all | solution.py:37
  318.1 0.3 convert_reduce_fusion.1
  318.3 0.6 copy-done.4
  319.0 0.4 multiply_reduce_fusion
  319.4 0.2 multiply_reduce_fusion.18
  319.9 0.1 stack.139
  320.1 2.5 collective-permute-start.2
  322.6 1.3 collective-permute-start.3
  323.9 1.0 broadcast_in_dim.2
  324.9 9.7 %all-to-all-start.2 = ((bf16[16,3,3,3,512]{4,3,2,1,0:T(4,128)(2,1)}), bf16[16,3,3,3,512]{4,3,2,1,0:T(4,128)(2,1)S(1)}, u32[]{:S(2)}, u32[]{:S(2)}) async-start(bf16[16,3,3,3,512]{4,3,2,1,0:T(4,128)(2,1)} %broadcast_in_dim.2), calls=%async_computation.2 | async-start | bytes 1179648 | tf_op jit(solution)/shard_map/all_to_all | solution.py:43
  334.9 0.0 copy-start.52
  334.9 5.9 %fusion.15 = bf16[512,896]{1,0:T(8,128)(2,1)} fusion(bf16[2048,512]{1,0:T(8,128)(2,1)} %bitcast.43, bf16[2048,2688]{1,0:T(8,128)(2,1)} %all-gather.5.cloned.1.call-done), kind=kOutput, calls=%fused_computation.63 | convolution fusion | flops 1879506944 | bytes 6684672 | tf_op jit(solution)/shard_map/dot_general | solution.py:129
  341.1 1.3 fusion.80
  342.4 11.5 %all-to-all-done.2 = bf16[16,3,3,3,512]{4,3,2,1,0:T(4,128)(2,1)S(1)} async-done(((bf16[16,3,3,3,512]{4,3,2,1,0:T(4,128)(2,1)}), bf16[16,3,3,3,512]{4,3,2,1,0:T(4,128)(2,1)S(1)}, u32[]{:S(2)}, u32[]{:S(2)}) %all-to-all-start.2) | async-done | bytes 442400 | tf_op jit(solution)/shard_map/all_to_all | solution.py:43
  353.9 0.8 convert_reduce_fusion.2
  (136 shorter events, 0.4 us)
Async XLA Ops:
  7.2 124.3 %copy-start = (bf16[896,512]{1,0:T(8,128)(2,1)S(1)}, bf16[896,512]{1,0:T(8,128)(2,1)}, u32[]{:S(2)}) copy-start(bf16[896,512]{1,0:T(8,128)(2,1)} %param.15) | copy-start | bytes 2752516
  7.2 16.3 %copy-start.3 = (bf16[2,8,8,512]{3,2,1,0:T(8,128)(2,1)S(1)}, bf16[2,8,8,512]{3,2,1,0:T(8,128)(2,1)}, u32[]{:S(2)}) copy-start(bf16[2,8,8,512]{3,2,1,0:T(8,128)(2,1)} %param.9) | copy-start | bytes 393220
  7.2 120.1 %all-gather.3.cloned.1.call-start = ((), (), s32[]{:S(2)}) async-start(), calls=%async_computation.3 | async-start | bytes 4456448 | tf_op jit(solution)/shard_map/all_gather | solution.py:26
  8.2 8.4 %collective-permute-start = (bf16[1,8,8,512]{3,2,1,0:T(8,128)(2,1)S(1)}, bf16[1,8,8,512]{3,2,1,0:T(8,128)(2,1)S(1)}, u32[]{:S(2)}, u32[]{:S(2)}) collective-permute-start(bf16[1,8,8,512]{3,2,1,0:T(8,128)(2,1)S(1)} %get-tuple-element.41), channel_id=1, source_target_pairs={{0,16},{16,32},{32,48},{48,64},{64,80},{80,96},{96,112},{112,128},... | collective-permute-start | bytes 196616 | tf_op jit(solution)/shard_map/ppermute | solution.py:14
  13.3 7.7 %collective-permute-start.1 = (bf16[1,8,8,512]{3,2,1,0:T(8,128)(2,1)S(1)}, bf16[1,8,8,512]{3,2,1,0:T(8,128)(2,1)S(1)}, u32[]{:S(2)}, u32[]{:S(2)}) collective-permute-start(bf16[1,8,8,512]{3,2,1,0:T(8,128)(2,1)S(1)} %get-tuple-element.42), channel_id=1, source_target_pairs={{16,0},{32,16},{48,32},{64,48},{80,64},{96,80},{112,96},{128,112},... | collective-permute-start | bytes 196616 | tf_op jit(solution)/shard_map/ppermute | solution.py:15
  15.5 115.7 %copy-start.7 = (f32[1,1,1,512]{3,2,1,0:T(1,128)}, f32[1,1,1,512]{3,2,1,0:T(1,128)S(1)}, u32[]{:S(2)}) copy-start(f32[1,1,1,512]{3,2,1,0:T(1,128)S(1)} %get-tuple-element.47) | copy-start | bytes 6148
  15.6 115.7 %copy-start.9 = (f32[1,1,1,512]{3,2,1,0:T(1,128)}, f32[1,1,1,512]{3,2,1,0:T(1,128)S(1)}, u32[]{:S(2)}) copy-start(f32[1,1,1,512]{3,2,1,0:T(1,128)S(1)} %get-tuple-element.48) | copy-start | bytes 6148
  15.6 115.7 %copy-start.11 = (f32[1,1,1,512]{3,2,1,0:T(1,128)}, f32[1,1,1,512]{3,2,1,0:T(1,128)S(1)}, u32[]{:S(2)}) copy-start(f32[1,1,1,512]{3,2,1,0:T(1,128)S(1)} %get-tuple-element.49) | copy-start | bytes 6148
  15.6 115.7 %copy-start.13 = (f32[1,1,1,512]{3,2,1,0:T(1,128)}, f32[1,1,1,512]{3,2,1,0:T(1,128)S(1)}, u32[]{:S(2)}) copy-start(f32[1,1,1,512]{3,2,1,0:T(1,128)S(1)} %get-tuple-element.50) | copy-start | bytes 6148
  15.6 115.7 %copy-start.15 = (f32[1,1,1,512]{3,2,1,0:T(1,128)}, f32[1,1,1,512]{3,2,1,0:T(1,128)S(1)}, u32[]{:S(2)}) copy-start(f32[1,1,1,512]{3,2,1,0:T(1,128)S(1)} %get-tuple-element.51) | copy-start | bytes 6148
  15.6 115.7 %copy-start.17 = (f32[1,1,1,512]{3,2,1,0:T(1,128)}, f32[1,1,1,512]{3,2,1,0:T(1,128)S(1)}, u32[]{:S(2)}) copy-start(f32[1,1,1,512]{3,2,1,0:T(1,128)S(1)} %get-tuple-element.52) | copy-start | bytes 6148
  15.6 115.7 %copy-start.19 = (f32[1,1,1,512]{3,2,1,0:T(1,128)}, f32[1,1,1,512]{3,2,1,0:T(1,128)S(1)}, u32[]{:S(2)}) copy-start(f32[1,1,1,512]{3,2,1,0:T(1,128)S(1)} %get-tuple-element.53) | copy-start | bytes 6148
  15.6 115.7 %copy-start.21 = (f32[1,1,1,512]{3,2,1,0:T(1,128)}, f32[1,1,1,512]{3,2,1,0:T(1,128)S(1)}, u32[]{:S(2)}) copy-start(f32[1,1,1,512]{3,2,1,0:T(1,128)S(1)} %get-tuple-element.54) | copy-start | bytes 6148
  15.6 115.7 %copy-start.23 = (f32[1,1,1,512]{3,2,1,0:T(1,128)}, f32[1,1,1,512]{3,2,1,0:T(1,128)S(1)}, u32[]{:S(2)}) copy-start(f32[1,1,1,512]{3,2,1,0:T(1,128)S(1)} %get-tuple-element.55) | copy-start | bytes 6148
  15.6 115.7 %copy-start.25 = (f32[1,1,1,512]{3,2,1,0:T(1,128)}, f32[1,1,1,512]{3,2,1,0:T(1,128)S(1)}, u32[]{:S(2)}) copy-start(f32[1,1,1,512]{3,2,1,0:T(1,128)S(1)} %get-tuple-element.56) | copy-start | bytes 6148
  15.6 115.7 %copy-start.27 = (f32[1,1,1,512]{3,2,1,0:T(1,128)}, f32[1,1,1,512]{3,2,1,0:T(1,128)S(1)}, u32[]{:S(2)}) copy-start(f32[1,1,1,512]{3,2,1,0:T(1,128)S(1)} %get-tuple-element.57) | copy-start | bytes 6148
  15.7 115.7 %copy-start.29 = (f32[1,1,1,512]{3,2,1,0:T(1,128)}, f32[1,1,1,512]{3,2,1,0:T(1,128)S(1)}, u32[]{:S(2)}) copy-start(f32[1,1,1,512]{3,2,1,0:T(1,128)S(1)} %get-tuple-element.58) | copy-start | bytes 6148
  15.7 115.7 %copy-start.31 = (f32[1,1,1,512]{3,2,1,0:T(1,128)}, f32[1,1,1,512]{3,2,1,0:T(1,128)S(1)}, u32[]{:S(2)}) copy-start(f32[1,1,1,512]{3,2,1,0:T(1,128)S(1)} %get-tuple-element.59) | copy-start | bytes 6148
  15.7 115.7 %copy-start.33 = (f32[1,1,1,512]{3,2,1,0:T(1,128)}, f32[1,1,1,512]{3,2,1,0:T(1,128)S(1)}, u32[]{:S(2)}) copy-start(f32[1,1,1,512]{3,2,1,0:T(1,128)S(1)} %get-tuple-element.60) | copy-start | bytes 6148
  15.7 115.7 %copy-start.35 = (f32[1,1,1,512]{3,2,1,0:T(1,128)}, f32[1,1,1,512]{3,2,1,0:T(1,128)S(1)}, u32[]{:S(2)}) copy-start(f32[1,1,1,512]{3,2,1,0:T(1,128)S(1)} %get-tuple-element.61) | copy-start | bytes 6148
  16.5 114.8 %copy-start.37 = (f32[1,1,1,512]{3,2,1,0:T(1,128)}, f32[1,1,1,512]{3,2,1,0:T(1,128)S(1)}, u32[]{:S(2)}) copy-start(f32[1,1,1,512]{3,2,1,0:T(1,128)S(1)} %get-tuple-element.62) | copy-start | bytes 6148
  16.5 114.8 %copy-start.39 = (f32[1,1,1,512]{3,2,1,0:T(1,128)}, f32[1,1,1,512]{3,2,1,0:T(1,128)S(1)}, u32[]{:S(2)}) copy-start(f32[1,1,1,512]{3,2,1,0:T(1,128)S(1)} %get-tuple-element.63) | copy-start | bytes 6148
  16.6 114.8 %copy-start.41 = (f32[1,1,1,512]{3,2,1,0:T(1,128)}, f32[1,1,1,512]{3,2,1,0:T(1,128)S(1)}, u32[]{:S(2)}) copy-start(f32[1,1,1,512]{3,2,1,0:T(1,128)S(1)} %get-tuple-element.64) | copy-start | bytes 6148
  16.6 114.8 %copy-start.43 = (f32[1,1,1,512]{3,2,1,0:T(1,128)}, f32[1,1,1,512]{3,2,1,0:T(1,128)S(1)}, u32[]{:S(2)}) copy-start(f32[1,1,1,512]{3,2,1,0:T(1,128)S(1)} %get-tuple-element.65) | copy-start | bytes 6148
  16.6 114.8 %copy-start.45 = (f32[1,1,1,512]{3,2,1,0:T(1,128)}, f32[1,1,1,512]{3,2,1,0:T(1,128)S(1)}, u32[]{:S(2)}) copy-start(f32[1,1,1,512]{3,2,1,0:T(1,128)S(1)} %get-tuple-element.66) | copy-start | bytes 6148
  16.6 114.8 %copy-start.47 = (f32[1,1,1,512]{3,2,1,0:T(1,128)}, f32[1,1,1,512]{3,2,1,0:T(1,128)S(1)}, u32[]{:S(2)}) copy-start(f32[1,1,1,512]{3,2,1,0:T(1,128)S(1)} %get-tuple-element.67) | copy-start | bytes 6148
  16.6 114.8 %copy-start.49 = (f32[1,1,1,512]{3,2,1,0:T(1,128)}, f32[1,1,1,512]{3,2,1,0:T(1,128)S(1)}, u32[]{:S(2)}) copy-start(f32[1,1,1,512]{3,2,1,0:T(1,128)S(1)} %get-tuple-element.68) | copy-start | bytes 6148
  16.6 114.8 %copy-start.51 = (f32[1,1,1,512]{3,2,1,0:T(1,128)}, f32[1,1,1,512]{3,2,1,0:T(1,128)S(1)}, u32[]{:S(2)}) copy-start(f32[1,1,1,512]{3,2,1,0:T(1,128)S(1)} %get-tuple-element.69) | copy-start | bytes 6148
  24.2 223.0 %all-gather.5.cloned.1.call-start = ((), (), s32[]{:S(2)}) async-start(), calls=%async_computation.4 | async-start | bytes 11698176 | tf_op jit(solution)/shard_map/all_gather | solution.py:26
  181.8 65.5 %copy-start.54 = (bf16[512,896]{1,0:T(8,128)(2,1)S(1)}, bf16[512,896]{1,0:T(8,128)(2,1)}, u32[]{:S(2)}) copy-start(bf16[512,896]{1,0:T(8,128)(2,1)} %param.14) | copy-start | bytes 2752516
  183.0 68.9 %copy-start.55 = (bf16[512,896]{1,0:T(8,128)(2,1)S(1)}, bf16[512,896]{1,0:T(8,128)(2,1)}, u32[]{:S(2)}) copy-start(bf16[512,896]{1,0:T(8,128)(2,1)} %param.13) | copy-start | bytes 2752516
  256.3 61.7 %all-to-all-start.1 = ((bf16[16,128,512]{2,1,0:T(8,128)(2,1)}), bf16[16,128,512]{2,1,0:T(8,128)(2,1)S(1)}, u32[]{:S(2)}, u32[]{:S(2)}) async-start(bf16[16,128,512]{2,1,0:T(8,128)(2,1)} %bitcast.41), calls=%async_computation.1 | async-start | bytes 4194304 | tf_op jit(solution)/shard_map/all_to_all | solution.py:37
  320.1 20.7 %collective-permute-start.2 = (bf16[1,8,8,512]{3,2,1,0:T(8,128)(2,1)S(1)}, bf16[1,8,8,512]{3,2,1,0:T(8,128)(2,1)S(1)}, u32[]{:S(2)}, u32[]{:S(2)}) collective-permute-start(bf16[1,8,8,512]{3,2,1,0:T(8,128)(2,1)S(1)} %get-tuple-element.39), channel_id=1, source_target_pairs={{0,16},{16,32},{32,48},{48,64},{64,80},{80,96},{96,112},{112,128},... | collective-permute-start | bytes 196616 | tf_op jit(solution)/shard_map/ppermute | solution.py:14
  322.6 18.3 %collective-permute-start.3 = (bf16[1,8,8,512]{3,2,1,0:T(8,128)(2,1)S(1)}, bf16[1,8,8,512]{3,2,1,0:T(8,128)(2,1)S(1)}, u32[]{:S(2)}, u32[]{:S(2)}) collective-permute-start(bf16[1,8,8,512]{3,2,1,0:T(8,128)(2,1)S(1)} %get-tuple-element.40), channel_id=1, source_target_pairs={{16,0},{32,16},{48,32},{64,48},{80,64},{96,80},{112,96},{128,112},... | collective-permute-start | bytes 196616 | tf_op jit(solution)/shard_map/ppermute | solution.py:15
  324.9 29.0 %all-to-all-start.2 = ((bf16[16,3,3,3,512]{4,3,2,1,0:T(4,128)(2,1)}), bf16[16,3,3,3,512]{4,3,2,1,0:T(4,128)(2,1)S(1)}, u32[]{:S(2)}, u32[]{:S(2)}) async-start(bf16[16,3,3,3,512]{4,3,2,1,0:T(4,128)(2,1)} %broadcast_in_dim.2), calls=%async_computation.2 | async-start | bytes 1179648 | tf_op jit(solution)/shard_map/all_to_all | solution.py:43
  334.7 6.2 %copy-start.8 = (f32[1,1,1,512]{3,2,1,0:T(1,128)S(1)}, f32[1,1,1,512]{3,2,1,0:T(1,128)}, u32[]{:S(2)}) copy-start(f32[1,1,1,512]{3,2,1,0:T(1,128)} %copy-done.7) | copy-start | bytes 6148
  334.7 6.2 %copy-start.10 = (f32[1,1,1,512]{3,2,1,0:T(1,128)S(1)}, f32[1,1,1,512]{3,2,1,0:T(1,128)}, u32[]{:S(2)}) copy-start(f32[1,1,1,512]{3,2,1,0:T(1,128)} %copy-done.9) | copy-start | bytes 6148
  334.7 6.2 %copy-start.12 = (f32[1,1,1,512]{3,2,1,0:T(1,128)S(1)}, f32[1,1,1,512]{3,2,1,0:T(1,128)}, u32[]{:S(2)}) copy-start(f32[1,1,1,512]{3,2,1,0:T(1,128)} %copy-done.11) | copy-start | bytes 6148
  334.7 6.2 %copy-start.14 = (f32[1,1,1,512]{3,2,1,0:T(1,128)S(1)}, f32[1,1,1,512]{3,2,1,0:T(1,128)}, u32[]{:S(2)}) copy-start(f32[1,1,1,512]{3,2,1,0:T(1,128)} %copy-done.13) | copy-start | bytes 6148
  334.7 6.2 %copy-start.16 = (f32[1,1,1,512]{3,2,1,0:T(1,128)S(1)}, f32[1,1,1,512]{3,2,1,0:T(1,128)}, u32[]{:S(2)}) copy-start(f32[1,1,1,512]{3,2,1,0:T(1,128)} %copy-done.15) | copy-start | bytes 6148
  334.7 6.2 %copy-start.18 = (f32[1,1,1,512]{3,2,1,0:T(1,128)S(1)}, f32[1,1,1,512]{3,2,1,0:T(1,128)}, u32[]{:S(2)}) copy-start(f32[1,1,1,512]{3,2,1,0:T(1,128)} %copy-done.17) | copy-start | bytes 6148
  334.7 6.2 %copy-start.20 = (f32[1,1,1,512]{3,2,1,0:T(1,128)S(1)}, f32[1,1,1,512]{3,2,1,0:T(1,128)}, u32[]{:S(2)}) copy-start(f32[1,1,1,512]{3,2,1,0:T(1,128)} %copy-done.19) | copy-start | bytes 6148
  334.7 6.2 %copy-start.22 = (f32[1,1,1,512]{3,2,1,0:T(1,128)S(1)}, f32[1,1,1,512]{3,2,1,0:T(1,128)}, u32[]{:S(2)}) copy-start(f32[1,1,1,512]{3,2,1,0:T(1,128)} %copy-done.21) | copy-start | bytes 6148
  334.7 6.2 %copy-start.24 = (f32[1,1,1,512]{3,2,1,0:T(1,128)S(1)}, f32[1,1,1,512]{3,2,1,0:T(1,128)}, u32[]{:S(2)}) copy-start(f32[1,1,1,512]{3,2,1,0:T(1,128)} %copy-done.23) | copy-start | bytes 6148
  334.7 6.2 %copy-start.26 = (f32[1,1,1,512]{3,2,1,0:T(1,128)S(1)}, f32[1,1,1,512]{3,2,1,0:T(1,128)}, u32[]{:S(2)}) copy-start(f32[1,1,1,512]{3,2,1,0:T(1,128)} %copy-done.25) | copy-start | bytes 6148
  334.8 6.2 %copy-start.28 = (f32[1,1,1,512]{3,2,1,0:T(1,128)S(1)}, f32[1,1,1,512]{3,2,1,0:T(1,128)}, u32[]{:S(2)}) copy-start(f32[1,1,1,512]{3,2,1,0:T(1,128)} %copy-done.27) | copy-start | bytes 6148
  334.8 6.2 %copy-start.30 = (f32[1,1,1,512]{3,2,1,0:T(1,128)S(1)}, f32[1,1,1,512]{3,2,1,0:T(1,128)}, u32[]{:S(2)}) copy-start(f32[1,1,1,512]{3,2,1,0:T(1,128)} %copy-done.29) | copy-start | bytes 6148
  334.8 6.2 %copy-start.32 = (f32[1,1,1,512]{3,2,1,0:T(1,128)S(1)}, f32[1,1,1,512]{3,2,1,0:T(1,128)}, u32[]{:S(2)}) copy-start(f32[1,1,1,512]{3,2,1,0:T(1,128)} %copy-done.31) | copy-start | bytes 6148
  (16 other events, 79.1 us)
Sparse Core Ops, SparseCore 0:
  24.3 102.8 all-gather.2
  183.1 64.0 all-gather.4
where the time goes:
time: 362 us
  waiting for transfers between devices  224 us (62%)
  blocking collectives  46.9 us (13%)
  starting transfers between devices  29.5 us (8%)
  matrix products  28 us (8%)
  between operations  15.1 us (4%)
  local copies, waits for them, and re-layouts  10 us (3%)
  other arithmetic  8.01 us (2%)
    all_gather x2, waiting for transfers between devices, in_one_piece(): lax.all_gather(both, axis, axis=dim, tiled=True)  167 us
    all_to_all x1, blocking collectives, sum_at_owner(): blocks = lax.all_to_all(in_blocks(x, dim, peers), axis, 0, 0, tiled=True)  46.9 us
    all_to_all x1, waiting for transfers between devices, sum_at_owner(): blocks = lax.all_to_all(in_blocks(x, dim, peers), axis, 0, 0, tiled=True)  41 us
    all_to_all x1, waiting for transfers between devices, from_everyone(): lax.all_to_all(jnp.broadcast_to(x[None], (peers, *x.shape)), axis, 0, 0,...  11.5 us
    all_to_all x1, starting transfers between devices, from_everyone(): lax.all_to_all(jnp.broadcast_to(x[None], (peers, *x.shape)), axis, 0, 0,...  9.74 us
    all_to_all x1, starting transfers between devices, sum_at_owner(): blocks = lax.all_to_all(in_blocks(x, dim, peers), axis, 0, 0, tiled=True)  9.57 us
    ppermute x2, starting transfers between devices, padded(): before = lax.ppermute(last, axis, up)  7.56 us
  transfers between devices with their start and end apart: 8, of which 5 were waited for; matrix products, arithmetic and copies ran while one was open for 6% of the time, Pallas kernels for 0%

commit v1 on v0

--- a/solution.py
+++ b/solution.py
@@ -1,7 +1,364 @@
+import functools
+
 import jax
 import jax.numpy as jnp
 from jax import lax
+from jax.experimental import pallas as pl
+from jax.experimental.pallas import tpu as pltpu
 from jax.sharding import PartitionSpec as P
+
+MESH = pl.DeviceIdType.MESH
+BF = jnp.bfloat16
+F32 = jnp.float32
+
+
+class Sends:
+    def __init__(self, sems):
+        self.sems, self.made = sems, []
+
+    def go(self, src, dst, recv, device):
+        copy = pltpu.make_async_remote_copy(
+            src_ref=src,
+            dst_ref=dst,
+            send_sem=self.sems.at[len(self.made)],
+            recv_sem=recv,
+            device_id=device,
+            device_id_type=MESH,
+        )
+        copy.start()
+        self.made.append(copy)
+
+    def finish(self):
+        for copy in self.made:
+            copy.wait_send()
+
+
+def arrived(dst, recv, sem, device):
+    pltpu.make_async_remote_copy(
+        src_ref=dst, dst_ref=dst, send_sem=sem, recv_sem=recv, device_id=device, device_id_type=MESH
+    ).wait_recv()
+
+
+class Place:
+    def __init__(self):
+        r, c = lax.axis_index("row"), lax.axis_index("col")
+        self.r, self.c = r, c
+        self.z, self.h = r // 2, r % 2
+        self.x, self.l, self.k = c // 4, (c // 2) % 2, c % 2
+        self.zp, self.zm = ((r + 2) % 16, c), ((r + 14) % 16, c)
+        self.hp = (r + 1 - 2 * self.h, c)
+        self.xp, self.xm = (r, (c + 4) % 16), (r, (c + 12) % 16)
+        self.lp = (r, c + 2 - 4 * self.l)
+        self.kp = (r, c + 1 - 2 * self.k)
+
+    def slab(self, dz, other):
+        hh = self.h + other * (1 - 2 * self.h)
+        return ((self.z + dz + 8) % 8) * 2 + hh
+
+    def tile(self, dx, other, k=None):
+        ll = self.l + other * (1 - 2 * self.l)
+        return ((self.x + dx + 4) % 4) * 4 + ll * 2 + (self.k if k is None else k)
+
+
+def meet(peers):
+    barrier = pltpu.get_barrier_semaphore()
+    for peer in peers:
+        pl.semaphore_signal(barrier, inc=1, device_id=peer, device_id_type=MESH)
+    pl.semaphore_wait(barrier, len(peers))
+
+
+class RowGather:
+    def __init__(self, at, sends, buf, recv):
+        self.at, self.sends, self.buf, self.recv = at, sends, buf, recv
+
+    def start(self, own):
+        at = self.at
+        for peer, way in ((at.hp, 0), (at.zp, 0), (at.zm, 1)):
+            self.sends.go(own, self.buf.at[at.r], self.recv.at[way, at.r], peer)
+
+    def wait(self, j, way, rows=None):
+        ref = self.buf.at[j] if rows is None else self.buf.at[j, pl.ds(rows, 64)]
+        arrived(ref, self.recv.at[way, j], self.sends.sems.at[0], self.at.hp)
+
+    def pair(self):
+        at = self.at
+        j = at.slab(0, 1)
+        self.wait(j, 0)
+        for peer, way in ((at.zp, 0), (at.zm, 1)):
+            self.sends.go(self.buf.at[j], self.buf.at[j], self.recv.at[way, j], peer)
+        return [j]
+
+    def step(self, s, other):
+        at = self.at
+        if s == 4:
+            j = at.slab(4, other)
+            self.wait(j, 0, 0)
+            self.wait(j, 1, 64)
+            return [j]
+        got = []
+        for way, dz, peer in ((0, -s, at.zp), (1, s, at.zm)):
+            j = at.slab(dz, other)
+            self.wait(j, way)
+            ref = self.buf.at[j] if s < 3 else self.buf.at[j, pl.ds(64 * way, 64)]
+            self.sends.go(ref, ref, self.recv.at[way, j], peer)
+            got.append(j)
+        return got
+
+
+class ColGather:
+    def __init__(self, at, sends, buf, recv):
+        self.at, self.sends, self.buf, self.recv = at, sends, buf, recv
+
+    def start(self, own):
+        at = self.at
+        for peer, way in ((at.lp, 0), (at.xp, 0), (at.xm, 1), (at.kp, 0)):
+            self.sends.go(own, self.buf.at[at.c], self.recv.at[way, at.c], peer)
+
+    def wait(self, j, way, rows=None):
+        ref = self.buf.at[j] if rows is None else self.buf.at[j, pl.ds(rows, 64)]
+        arrived(ref, self.recv.at[way, j], self.sends.sems.at[0], self.at.kp)
+
+    def pair(self):
+        at = self.at
+        j = at.tile(0, 1)
+        self.wait(j, 0)
+        for peer, way in ((at.xp, 0), (at.xm, 1), (at.kp, 0)):
+            self.sends.go(self.buf.at[j], self.buf.at[j], self.recv.at[way, j], peer)
+
+    def step(self, s, other):
+        at = self.at
+        if s == 2:
+            j = at.tile(2, other)
+            self.wait(j, 0, 0)
+            self.wait(j, 1, 64)
+            self.sends.go(self.buf.at[j], self.buf.at[j], self.recv.at[0, j], at.kp)
+            return
+        for way, dx, peer in ((0, -1, at.xp), (1, 1, at.xm)):
+            j = at.tile(dx, other)
+            self.wait(j, way)
+            ref = self.buf.at[j, pl.ds(64 * way, 64)]
+            self.sends.go(ref, ref, self.recv.at[way, j], peer)
+            self.sends.go(self.buf.at[j], self.buf.at[j], self.recv.at[0, j], at.kp)
+
+    def rest(self):
+        for dx, other in ((0, 0), (0, 1), (1, 0), (1, 1), (-1, 0), (-1, 1), (2, 0), (2, 1)):
+            self.wait(self.at.tile(dx, other, 1 - self.at.k), 0)
+
+
+def front(
+    og, xin, gate, up, wd,
+    dy_all, x_all, g_all, u_all, dh_all,
+    wdt, part, mate, stage, xp_half, xm_half, xp_full, xm_full, y_full,
+    send_sem, dy_sem, x_sem, g_sem, u_sem, dh_sem, mate_sem, ring_sem,
+):
+    at = Place()
+    sends = Sends(send_sem)
+    meet((at.zp, at.zm, at.hp, at.xp, at.xm, at.lp, at.kp))
+    dy = RowGather(at, sends, dy_all, dy_sem)
+    xg = RowGather(at, sends, x_all, x_sem)
+    gg = ColGather(at, sends, g_all, g_sem)
+    ug = ColGather(at, sends, u_all, u_sem)
+    dg = ColGather(at, sends, dh_all, dh_sem)
+    dy.start(og)
+    gg.start(gate)
+    ug.start(up)
+    dy_all[at.r] = og[...]
+    g_all[at.c] = gate[...]
+    u_all[at.c] = up[...]
+    x_all[at.r] = xin[...]
+    wdt[...] = wd[...].T
+
+    def partial(j):
+        part[j] = jnp.dot(dy_all[j], wdt[...], preferred_element_type=F32).astype(BF)
+
+    def to_mate(zz):
+        j = zz * 2 + 1 - at.k
+        sends.go(part.at[j], mate.at[zz], mate_sem.at[zz], at.kp)
+
+    def zed(dz):
+        return (at.z + dz + 8) % 8
+
+    partial(at.r)
+    for j in dy.pair():
+        partial(j)
+    to_mate(at.z)
+    gg.pair()
+    ug.pair()
+    for s in (1, 2, 3):
+        for other in (0, 1):
+            for j in dy.step(s, other):
+                partial(j)
+            if s == 1:
+                gg.step(1, other)
+            elif s == 2:
+                gg.step(2, other)
+            else:
+                ug.step(1, other)
+        to_mate(zed(s))
+        to_mate(zed(-s))
+    for other in (0, 1):
+        for j in dy.step(4, other):
+            partial(j)
+    to_mate(zed(4))
+    xg.start(xin)
+    for other in (0, 1):
+        ug.step(2, other)
+    xg.pair()
+
+    def summed(xx, ll):
+        zz = xx * 2 + ll
+        arrived(mate.at[zz], mate_sem.at[zz], send_sem.at[0], at.kp)
+        return part[zz * 2 + at.k].astype(F32) + mate[zz].astype(F32)
+
+    def ex(dx):
+        return (at.x + dx + 4) % 4
+
+    for ll in (0, 1):
+        stage[0, ll] = summed(ex(2), ll).astype(BF)
+        sends.go(stage.at[0, ll, pl.ds(0, 64)], xp_half.at[ll], ring_sem.at[0, ll], at.xp)
+        sends.go(stage.at[0, ll, pl.ds(64, 64)], xm_half.at[ll], ring_sem.at[1, ll], at.xm)
+    for other in (0, 1):
+        xg.step(1, other)
+    for ll in (0, 1):
+        total = summed(ex(1), ll)
+        arrived(xp_half.at[ll], ring_sem.at[0, ll], send_sem.at[0], at.xm)
+        stage[1, ll, 0:64] = (total[0:64] + xp_half[ll].astype(F32)).astype(BF)
+        stage[1, ll, 64:128] = total[64:128].astype(BF)
+        sends.go(stage.at[1, ll], xp_full.at[ll], ring_sem.at[2, ll], at.xp)
+        total = summed(ex(-1), ll)
+        arrived(xm_half.at[ll], ring_sem.at[1, ll], send_sem.at[0], at.xp)
+        stage[2, ll, 0:64] = total[0:64].astype(BF)
+        stage[2, ll, 64:128] = (total[64:128] + xm_half[ll].astype(F32)).astype(BF)
+        sends.go(stage.at[2, ll], xm_full.at[ll], ring_sem.at[3, ll], at.xm)
+    for other in (0, 1):
+        xg.step(2, other)
+
+    def whole(ll, which):
+        total = summed(at.x, ll)
+        arrived(xp_full.at[ll], ring_sem.at[2, ll], send_sem.at[0], at.xm)
+        arrived(xm_full.at[ll], ring_sem.at[3, ll], send_sem.at[0], at.xp)
+        return total + xp_full[ll].astype(F32) + xm_full[ll].astype(F32)
+
+    stage[3, 0] = whole(1 - at.l, 0).astype(BF)
+    sends.go(stage.at[3, 0], y_full, ring_sem.at[4, 0], at.lp)
+    mine = whole(at.l, 1)
+    arrived(y_full, ring_sem.at[4, 0], send_sem.at[0], at.lp)
+    dh_all[at.c] = (mine + y_full[...].astype(F32)).astype(BF)
+    dg.start(dh_all.at[at.c])
+    for other in (0, 1):
+        xg.step(3, other)
+    dg.pair()
+    for other in (0, 1):
+        dg.step(1, other)
+    for other in (0, 1):
+        dg.step(2, other)
+    for other in (0, 1):
+        xg.step(4, other)
+    gg.rest()
+    ug.rest()
+    dg.rest()
+    sends.finish()
+
+
+def back(og, parts, out, stage, half, full, pair, send_sem, ring_sem):
+    at = Place()
+    sends = Sends(send_sem)
+    meet((at.zp, at.zm, at.hp))
+    for other in (0, 1):
+        j = at.slab(4, other)
+        for way, peer in ((0, at.zp), (1, at.zm)):
+            rows = pl.ds(64 * way, 64)
+            sends.go(parts.at[j, rows], half.at[way, other], ring_sem.at[0, way, other], peer)
+    for t in (1, 2, 3):
+        for other in (0, 1):
+            for way, peer, source in ((0, at.zp, at.zm), (1, at.zm, at.zp)):
+                j = at.slab((4 - t) * (1 - 2 * way), other)
+                held = stage.at[t - 1, way, other]
+                if t == 1:
+                    lo = 64 * way
+                    arrived(half.at[way, other], ring_sem.at[0, way, other], send_sem.at[0], source)
+                    held[lo : lo + 64] = (
+                        parts[j, lo : lo + 64].astype(F32) + half[way, other].astype(F32)
+                    ).astype(BF)
+                    held[64 - lo : 128 - lo] = parts[j, 64 - lo : 128 - lo]
+                else:
+                    came = full.at[t - 2, way, other]
+                    arrived(came, ring_sem.at[t - 1, way, other], send_sem.at[0], source)
+                    held[...] = (parts[j].astype(F32) + came[...].astype(F32)).astype(BF)
+                sends.go(held, full.at[t - 1, way, other], ring_sem.at[t, way, other], peer)
+
+    def whole(other):
+        j = at.slab(0, other)
+        total = parts[j].astype(F32)
+        for way, source in ((0, at.zm), (1, at.zp)):
+            came = full.at[2, way, other]
+            arrived(came, ring_sem.at[3, way, other], send_sem.at[0], source)
+            total = total + came[...].astype(F32)
+        return total
+
+    pair[0] = whole(1).astype(BF)
+    sends.go(pair.at[0], pair.at[1], ring_sem.at[4, 0, 0], at.hp)
+    mine = og[...].astype(F32) + whole(0)
+    arrived(pair.at[1], ring_sem.at[4, 0, 0], send_sem.at[0], at.hp)
+    out[...] = mine + pair[1].astype(F32)
+    sends.finish()
+
+
+VM = pl.BlockSpec(memory_space=pltpu.VMEM)
+DMA = pltpu.SemaphoreType.DMA
+
+
+def run_front(og, xin, gate, up, wd):
+    feats, units = og.shape[1], gate.shape[1]
+    tok = (16, 128, feats)
+    hid = (16, 128, units)
+    return pl.pallas_call(
+        front,
+        out_shape=[jax.ShapeDtypeStruct(s, BF) for s in (tok, tok, hid, hid, hid)],
+        in_specs=[VM] * 5,
+        out_specs=[VM] * 5,
+        scratch_shapes=[
+            pltpu.VMEM((feats, units), BF),
+            pltpu.VMEM(hid, BF),
+            pltpu.VMEM((8, 128, units), BF),
+            pltpu.VMEM((4, 2, 128, units), BF),
+            pltpu.VMEM((2, 64, units), BF),
+            pltpu.VMEM((2, 64, units), BF),
+            pltpu.VMEM((2, 128, units), BF),
+            pltpu.VMEM((2, 128, units), BF),
+            pltpu.VMEM((128, units), BF),
+            DMA((120,)),
+            DMA((2, 16)),
+            DMA((2, 16)),
+            DMA((2, 16)),
+            DMA((2, 16)),
+            DMA((2, 16)),
+            DMA((8,)),
+            DMA((5, 2)),
+        ],
+        compiler_params=pltpu.CompilerParams(collective_id=0, has_side_effects=True),
+        name="front",
+    )(og, xin, gate, up, wd)
+
+
+def run_back(og, parts):
+    feats = og.shape[1]
+    return pl.pallas_call(
+        back,
+        out_shape=jax.ShapeDtypeStruct((128, feats), F32),
+        in_specs=[VM] * 2,
+        out_specs=VM,
+        scratch_shapes=[
+            pltpu.VMEM((3, 2, 2, 128, feats), BF),
+            pltpu.VMEM((2, 2, 64, feats), BF),
+            pltpu.VMEM((3, 2, 2, 128, feats), BF),
+            pltpu.VMEM((2, 128, feats), BF),
+            DMA((20,)),
+            DMA((5, 2, 2)),
+        ],
+        compiler_params=pltpu.CompilerParams(collective_id=1, has_side_effects=True),
+        name="back",
+    )(og, parts)
 
 
 def padded(x, sides, width):
@@ -15,27 +372,6 @@
         after = lax.ppermute(first, axis, down)
         x = jnp.concatenate([before, x, after], axis=dim)
     return x
-
-
-def in_one_piece(arrays, axis, dim, along):
-    ends, at = ([], 0)
-    for a in arrays[:-1]:
-        at += a.shape[along]
-        ends.append(at)
-    both = jnp.concatenate(arrays, axis=along)
-    return tuple(jnp.split(lax.all_gather(both, axis, axis=dim, tiled=True), ends, axis=along))
-
-
-def in_blocks(x, dim, peers):
-    dims = x.shape
-    blocks = x.reshape(*dims[:dim], peers, dims[dim] // peers, *dims[dim + 1 :])
-    return jnp.moveaxis(blocks, dim, 0)
-
-
-def sum_at_owner(x, axis, dim):
-    peers = lax.axis_size(axis)
-    blocks = lax.all_to_all(in_blocks(x, dim, peers), axis, 0, 0, tiled=True)
-    return jnp.sum(blocks.astype(jnp.float32), axis=0)
 
 
 def from_everyone(x, axis):
@@ -106,19 +442,23 @@
     mixed_in = (patches.astype(jnp.float32) + correlate(framed_in, conv_kernel, False)).astype(
         jnp.bfloat16
     )
-    whole_in, whole_grad = in_one_piece((mixed_in, out_grad), "row", 0, 1)
-    all_rows = whole_in.shape[0] * height * breadth
-    flat_in = whole_in.reshape(all_rows, features)
-    flat_grad = whole_grad.reshape(all_rows, features)
+    own = planes * height * breadth
+    og = out_grad.reshape(own, features)
+    flat_grad, flat_in, gate_all, up_all, hidden_grad = (
+        a.reshape(16 * own, a.shape[2])
+        for a in run_front(og, mixed_in.reshape(own, features), saved_gate, saved_up, w_down)
+    )
     contract_cols = (((1,), (1,)), ((), ()))
     contract_rows = (((0,), (0,)), ((), ()))
-    partial_value = lax.dot_general(
-        flat_grad, w_down, contract_cols, preferred_element_type=jnp.float32
-    )
-    hidden_grad = sum_at_owner(partial_value.astype(jnp.bfloat16), "col", 0)
-    hidden_act, gate_grad, up_grad = swiglu_back(hidden_grad, saved_gate, saved_up)
-    hidden_all, gate_grad_all, up_grad_all = in_one_piece(
-        (hidden_act, gate_grad, up_grad), "col", 0, 1
+    hidden_all, gate_grad_all, up_grad_all = swiglu_back(
+        hidden_grad.astype(jnp.float32), gate_all, up_all
+    )
+    term = lax.dot_general(gate_grad_all, w_gate, contract_cols, preferred_element_type=jnp.float32)
+    term = term + lax.dot_general(
+        up_grad_all, w_up, contract_cols, preferred_element_type=jnp.float32
+    )
+    total_grad = run_back(og, term.astype(jnp.bfloat16).reshape(16, own, features)).reshape(
+        planes, height, breadth, features
     )
     down_wgrad = lax.dot_general(
         hidden_all, flat_grad, contract_rows, preferred_element_type=jnp.float32
@@ -129,16 +469,6 @@
     up_wgrad = lax.dot_general(
         flat_in, up_grad_all, contract_rows, preferred_element_type=jnp.float32
     ).astype(jnp.bfloat16)
-    term = lax.dot_general(gate_grad_all, w_gate, contract_cols, preferred_element_type=jnp.float32)
-    mlp_grad = sum_at_owner(
-        (
-            term
-            + lax.dot_general(up_grad_all, w_up, contract_cols, preferred_element_type=jnp.float32)
-        ).astype(jnp.bfloat16),
-        "row",
-        0,
-    )
-    total_grad = out_grad.astype(jnp.float32) + mlp_grad.reshape(planes, height, breadth, features)
     grad_rimmed = padded(total_grad.astype(jnp.bfloat16), (("row", 0),), 1).astype(total_grad.dtype)
     patch_grad = (total_grad + correlate(frame_sides(grad_rimmed), conv_kernel, True)).astype(
         jnp.bfloat16

time: 362 us -> 207 us (0.57)
  waiting for transfers between devices: 224 us -> 14.9 us
  Pallas kernels: 0 us -> 125 us
  blocking collectives: 46.9 us -> 0 us
  between operations: 15.1 us -> 1 us
  starting transfers between devices: 29.5 us -> 20.7 us
  other arithmetic: 8.01 us -> 14.9 us
  local copies, waits for them, and re-layouts: 10 us -> 4.74 us
    all_gather x2 -> x0, waiting for transfers between devices: 167 us -> none  [in_one_piece(): lax.all_gather(both, axis, axis=dim, tiled=True)]
    pallas_call x0 -> x2, Pallas kernels: none -> 125 us  [the longest x1 91.9 us: run_front(): pl.pallas_call(front, out_shape=[jax.ShapeDtypeStruct(s, BF) for s in (to...]
    all_to_all x1 -> x0, blocking collectives: 46.9 us -> none  [sum_at_owner(): blocks = lax.all_to_all(in_blocks(x, dim, peers), axis, 0, 0, tiled=True)]
    all_to_all x1 -> x0, waiting for transfers between devices: 41 us -> none  [sum_at_owner(): blocks = lax.all_to_all(in_blocks(x, dim, peers), axis, 0, 0, tiled=True)]
    all_to_all x1 -> x0, starting transfers between devices: 9.57 us -> none  [sum_at_owner(): blocks = lax.all_to_all(in_blocks(x, dim, peers), axis, 0, 0, tiled=True)]
    convert_element_type x1 -> x2, other arithmetic: 0.3 us -> 7.01 us  [the longest x1 6.77 us: swiglu_back(): up_grad = (hidden_grad * silu_g).astype(jnp.bfloat16)]
    split x1 -> x0, local copies, waits for them, and re-layouts: 3.95 us -> none  [in_one_piece(): jnp.split(lax.all_gather(both, axis, axis=dim, tiled=True), ends, axis=al...]
  transfers between devices with their start and end apart: 8 -> 5, of which waited for: 5 -> 2; matrix products, arithmetic and copies ran while one was open for 6% -> 5% of each run, Pallas kernels for 0% -> 0%
where the time goes in v1:
time: 207 us
  Pallas kernels  125 us (60%)
  matrix products  25.6 us (12%)
  starting transfers between devices  20.7 us (10%)
  waiting for transfers between devices  14.9 us (7%)
  other arithmetic  14.9 us (7%)
  local copies, waits for them, and re-layouts  4.74 us (2%)
    pallas_call x1, Pallas kernels, run_front(): pl.pallas_call(front, out_shape=[jax.ShapeDtypeStruct(s, BF) for s in (to...  91.9 us
    pallas_call x1, Pallas kernels, run_back(): pl.pallas_call(back, out_shape=jax.ShapeDtypeStruct((128, feats), F32), i...  33.2 us
    all_to_all x1, waiting for transfers between devices, from_everyone(): lax.all_to_all(jnp.broadcast_to(x[None], (peers, *x.shape)), axis, 0, 0,...  10.3 us
    all_to_all x1, starting transfers between devices, from_everyone(): lax.all_to_all(jnp.broadcast_to(x[None], (peers, *x.shape)), axis, 0, 0,...  9.16 us
    ppermute x2, starting transfers between devices, padded(): before = lax.ppermute(last, axis, up)  8.91 us
    dot_general x1, matrix products, body(): lax.dot_general(flat_in, up_grad_all, contract_rows, preferred_element_ty...  7.31 us
    dot_general x1, matrix products, body(): lax.dot_general(hidden_all, flat_grad, contract_rows, preferred_element_t...  7.11 us
    convert_element_type x1, other arithmetic, swiglu_back(): up_grad = (hidden_grad * silu_g).astype(jnp.bfloat16)  6.77 us
  transfers between devices with their start and end apart: 5, of which 2 were waited for; matrix products, arithmetic and copies ran while one was open for 5% of the time, Pallas kernels for 0%

profile of v1, /device:TPU:2, one launch (start us, length us, event | category | flops | bytes accessed | tf_op | source)
XLA Modules:
  0.0 206.8 jit_solution(5541295859119119031)
XLA Ops:
  0.6 0.0 copy-start
  0.6 1.0 fusion.83
  1.6 5.1 %collective-permute-start = (bf16[1,8,8,512]{3,2,1,0:T(8,128)(2,1)S(1)}, bf16[1,8,8,512]{3,2,1,0:T(8,128)(2,1)S(1)}, u32[]{:S(2)}, u32[]{:S(2)}) collective-permute-start(bf16[1,8,8,512]{3,2,1,0:T(8,128)(2,1)S(1)} %get-tuple-element.46), channel_id=1, source_target_pairs={{0,16},{16,32},{32,48},{48,64},{64,80},{80,96},{96,112},{112,128},... | collective-permute-start | bytes 196616 | tf_op jit(solution)/shard_map/ppermute | solution.py:371
  6.7 1.3 collective-permute-start.1
  8.0 0.9 fusion.84
  8.9 0.8 fusion.85
  9.8 0.0 collective-permute-done
  9.8 4.6 %collective-permute-done.1 = bf16[1,8,8,512]{3,2,1,0:T(8,128)(2,1)S(1)} collective-permute-done((bf16[1,8,8,512]{3,2,1,0:T(8,128)(2,1)S(1)}, bf16[1,8,8,512]{3,2,1,0:T(8,128)(2,1)S(1)}, u32[]{:S(2)}, u32[]{:S(2)}) %collective-permute-start.1) | collective-permute-done | bytes 65568 | tf_op jit(solution)/shard_map/ppermute | solution.py:372
  14.4 0.9 maximum_convert_fusion
  15.3 2.2 %add_convert_fusion.1 = bf16[2,8,8,512]{3,2,1,0:T(8,128)(2,1)} fusion(bf16[2,8,8,512]{3,2,1,0:T(8,128)(2,1)} %param.8, f32[4,8,8,512]{3,2,1,0:T(8,128)S(1)} %maximum_convert_fusion, f32[512]{0:T(512)S(1)} %bitcast.160, f32[512]{0:T(512)S(1)} %bitcast.162, f32[512]{0:T(512)S(1)} %bitcast.112, f32[512]{0:T(512)S(1)} %bitcast.114, f32[512]{0:T(512)S(1)} %bitcast.116, ...), kind=kLoop, calls=%fused_computation.167 | loop fusion | flops 3670016 | bytes 1628160 | tf_op jit(solution)/shard_map/convert_element_type | solution.py:442
  17.5 91.9 %front.1 = (bf16[16,128,512]{2,1,0:T(8,128)(2,1)}, bf16[16,128,512]{2,1,0:T(8,128)(2,1)}, bf16[16,128,896]{2,1,0:T(8,128)(2,1)}, bf16[16,128,896]{2,1,0:T(8,128)(2,1)}, bf16[16,128,896]{2,1,0:T(8,128)(2,1)}) custom-call(bf16[128,512]{1,0:T(8,128)(2,1)} %bitcast.107, bf16[128,512]{1,0:T(8,128)(2,1)} %bitcast.109, bf16[128,896]{1,0:T(8,128)(2,1)} %gate.1, ...), custom_call_target="tpu_custom_call" | custom-call | tf_op jit(solution)/shard_map/front/pallas_call | solution.py:315
  109.4 6.8 %fusion.13 = (bf16[2048,896]{1,0:T(8,128)(2,1)S(1)}, bf16[2048,896]{1,0:T(8,128)(2,1)S(1)}) fusion(bf16[16,128,896]{2,1,0:T(8,128)(2,1)} %get-tuple-element.12, bf16[16,128,896]{2,1,0:T(8,128)(2,1)} %get-tuple-element.10, bf16[16,128,896]{2,1,0:T(8,128)(2,1)} %get-tuple-element.11), kind=kLoop, calls=%fused_computation.67 | loop fusion | flops 29360128 | bytes 18350080 | tf_op jit(solution)/shard_map/convert_element_type | solution.py:434
  116.2 0.0 copy-done
  116.2 0.0 copy-start.6
  116.2 2.4 %fusion.86 = f32[2048,512]{1,0:T(8,128)S(1)} fusion(bf16[2048,896]{1,0:T(8,128)(2,1)S(1)} %get-tuple-element.43, bf16[512,896]{1,0:T(8,128)(2,1)S(1)} %copy-done), kind=kOutput, calls=%fused_computation.176 | convolution fusion | flops 1879048192 | bytes 8781824 | tf_op jit(solution)/shard_map/dot_general | solution.py:456
  118.6 0.0 copy-done.6
  118.6 3.8 %add_convert_fusion = bf16[2048,512]{1,0:T(8,128)(2,1)} fusion(f32[2048,512]{1,0:T(8,128)S(1)} %fusion.86, bf16[2048,896]{1,0:T(8,128)(2,1)S(1)} %get-tuple-element.42, bf16[512,896]{1,0:T(8,128)(2,1)S(1)} %copy-done.6), kind=kOutput, calls=%fused_computation.75 | convolution fusion | flops 1881145344 | bytes 10878976 | tf_op jit(solution)/shard_map/dot_general | solution.py:457
  122.4 33.2 %back.1 = f32[128,512]{1,0:T(8,128)} custom-call(bf16[128,512]{1,0:T(8,128)(2,1)} %bitcast.108, bf16[16,128,512]{2,1,0:T(8,128)(2,1)} %bitcast.106), custom_call_target="tpu_custom_call" | custom-call | tf_op jit(solution)/shard_map/back/pallas_call | solution.py:346
  155.6 1.2 multiply_reduce_fusion.1
  156.8 1.4 multiply_reduce_fusion
  158.2 0.0 copy-start.2
  158.2 0.0 copy-start.3
  158.2 0.0 copy-start.4
  158.3 0.0 copy-start.5
  158.3 7.1 %bitcast_convert_fusion = bf16[896,512]{1,0:T(8,128)(2,1)} fusion(bf16[16,128,512]{2,1,0:T(8,128)(2,1)} %get-tuple-element.14, bf16[16,128,896]{2,1,0:T(8,128)(2,1)} %get-tuple-element.11, bf16[16,128,896]{2,1,0:T(8,128)(2,1)} %get-tuple-element.12), kind=kOutput, calls=%fused_computation.80 | convolution fusion | flops 1894187008 | bytes 10354688 | tf_op jit(solution)/shard_map/dot_general | solution.py:463
  165.4 0.0 copy-done.2
  165.4 0.0 copy-done.3
  165.4 0.0 copy-done.4
  165.4 0.7 copy-done.5
  166.1 0.0 copy-start.1
  166.1 4.9 %bitcast_convert_fusion.2 = bf16[512,896]{1,0:T(8,128)(2,1)} fusion(bf16[16,128,512]{2,1,0:T(8,128)(2,1)S(1)} %copy-done.5, bf16[16,128,896]{2,1,0:T(8,128)(2,1)S(1)} %copy-done.2, bf16[16,128,896]{2,1,0:T(8,128)(2,1)S(1)} %copy-done.3, bf16[16,128,896]{2,1,0:T(8,128)(2,1)S(1)} %copy-done.4), kind=kOutput, calls=%fused_computation.82 | convolution fusion | flops 1903362048 | bytes 14024704 | tf_op jit(solution)/shard_map/dot_general | solution.py:466
  171.3 0.1 stack.139
  171.5 0.0 copy-done.1
  171.5 0.2 convert_element_type.103
  171.8 3.8 %collective-permute-start.2 = (bf16[1,8,8,512]{3,2,1,0:T(8,128)(2,1)S(1)}, bf16[1,8,8,512]{3,2,1,0:T(8,128)(2,1)S(1)}, u32[]{:S(2)}, u32[]{:S(2)}) collective-permute-start(bf16[1,8,8,512]{3,2,1,0:T(8,128)(2,1)S(1)} %get-tuple-element.44), channel_id=1, source_target_pairs={{0,16},{16,32},{32,48},{48,64},{64,80},{80,96},{96,112},{112,128},... | collective-permute-start | bytes 196616 | tf_op jit(solution)/shard_map/ppermute | solution.py:371
  175.6 1.3 collective-permute-start.3
  176.9 1.0 broadcast_in_dim.2
  177.9 9.2 %all-to-all-start = ((bf16[16,3,3,3,512]{4,3,2,1,0:T(4,128)(2,1)}), bf16[16,3,3,3,512]{4,3,2,1,0:T(4,128)(2,1)S(1)}, u32[]{:S(2)}, u32[]{:S(2)}) async-start(bf16[16,3,3,3,512]{4,3,2,1,0:T(4,128)(2,1)} %broadcast_in_dim.2), calls=%async_computation | async-start | bytes 1179648 | tf_op jit(solution)/shard_map/all_to_all | solution.py:379
  187.0 7.3 %bitcast_convert_fusion.1 = bf16[512,896]{1,0:T(8,128)(2,1)} fusion(bf16[16,128,512]{2,1,0:T(8,128)(2,1)} %get-tuple-element.13, bf16[16,128,896]{2,1,0:T(8,128)(2,1)} %get-tuple-element.10, bf16[16,128,896]{2,1,0:T(8,128)(2,1)} %get-tuple-element.12), kind=kOutput, calls=%fused_computation.81 | convolution fusion | flops 1894187008 | bytes 10354688 | tf_op jit(solution)/shard_map/dot_general | solution.py:469
  194.3 0.0 collective-permute-done.2
  194.3 0.0 collective-permute-done.3
  194.4 1.3 fusion.78
  195.7 10.3 %all-to-all-done = bf16[16,3,3,3,512]{4,3,2,1,0:T(4,128)(2,1)S(1)} async-done(((bf16[16,3,3,3,512]{4,3,2,1,0:T(4,128)(2,1)}), bf16[16,3,3,3,512]{4,3,2,1,0:T(4,128)(2,1)S(1)}, u32[]{:S(2)}, u32[]{:S(2)}) %all-to-all-start) | async-done | bytes 442400 | tf_op jit(solution)/shard_map/all_to_all | solution.py:379
  206.0 0.8 convert_reduce_fusion
  (30 shorter events, 0.2 us)
Async XLA Ops:
  0.6 115.5 %copy-start = (bf16[512,896]{1,0:T(8,128)(2,1)S(1)}, bf16[512,896]{1,0:T(8,128)(2,1)}, u32[]{:S(2)}) copy-start(bf16[512,896]{1,0:T(8,128)(2,1)} %param.13) | copy-start | bytes 2752516
  1.6 8.2 %collective-permute-start = (bf16[1,8,8,512]{3,2,1,0:T(8,128)(2,1)S(1)}, bf16[1,8,8,512]{3,2,1,0:T(8,128)(2,1)S(1)}, u32[]{:S(2)}, u32[]{:S(2)}) collective-permute-start(bf16[1,8,8,512]{3,2,1,0:T(8,128)(2,1)S(1)} %get-tuple-element.46), channel_id=1, source_target_pairs={{0,16},{16,32},{32,48},{48,64},{64,80},{80,96},{96,112},{112,128},... | collective-permute-start | bytes 196616 | tf_op jit(solution)/shard_map/ppermute | solution.py:371
  6.7 7.7 %collective-permute-start.1 = (bf16[1,8,8,512]{3,2,1,0:T(8,128)(2,1)S(1)}, bf16[1,8,8,512]{3,2,1,0:T(8,128)(2,1)S(1)}, u32[]{:S(2)}, u32[]{:S(2)}) collective-permute-start(bf16[1,8,8,512]{3,2,1,0:T(8,128)(2,1)S(1)} %get-tuple-element.47), channel_id=1, source_target_pairs={{16,0},{32,16},{48,32},{64,48},{80,64},{96,80},{112,96},{128,112},... | collective-permute-start | bytes 196616 | tf_op jit(solution)/shard_map/ppermute | solution.py:372
  116.2 2.4 %copy-start.6 = (bf16[512,896]{1,0:T(8,128)(2,1)S(1)}, bf16[512,896]{1,0:T(8,128)(2,1)}, u32[]{:S(2)}) copy-start(bf16[512,896]{1,0:T(8,128)(2,1)} %param.14) | copy-start | bytes 2752516
  158.2 7.2 %copy-start.2 = (bf16[16,128,896]{2,1,0:T(8,128)(2,1)S(1)}, bf16[16,128,896]{2,1,0:T(8,128)(2,1)}, u32[]{:S(2)}) copy-start(bf16[16,128,896]{2,1,0:T(8,128)(2,1)} %get-tuple-element.12) | copy-start | bytes 11010052
  158.2 7.1 %copy-start.3 = (bf16[16,128,896]{2,1,0:T(8,128)(2,1)S(1)}, bf16[16,128,896]{2,1,0:T(8,128)(2,1)}, u32[]{:S(2)}) copy-start(bf16[16,128,896]{2,1,0:T(8,128)(2,1)} %get-tuple-element.10) | copy-start | bytes 11010052
  158.2 7.1 %copy-start.4 = (bf16[16,128,896]{2,1,0:T(8,128)(2,1)S(1)}, bf16[16,128,896]{2,1,0:T(8,128)(2,1)}, u32[]{:S(2)}) copy-start(bf16[16,128,896]{2,1,0:T(8,128)(2,1)} %get-tuple-element.11) | copy-start | bytes 11010052
  158.3 7.8 %copy-start.5 = (bf16[16,128,512]{2,1,0:T(8,128)(2,1)S(1)}, bf16[16,128,512]{2,1,0:T(8,128)(2,1)}, u32[]{:S(2)}) copy-start(bf16[16,128,512]{2,1,0:T(8,128)(2,1)} %get-tuple-element.13) | copy-start | bytes 6291460
  166.1 5.4 %copy-start.1 = (f32[128,512]{1,0:T(8,128)S(1)}, f32[128,512]{1,0:T(8,128)}, u32[]{:S(2)}) copy-start(f32[128,512]{1,0:T(8,128)} %back.1) | copy-start | bytes 786436
  171.8 22.5 %collective-permute-start.2 = (bf16[1,8,8,512]{3,2,1,0:T(8,128)(2,1)S(1)}, bf16[1,8,8,512]{3,2,1,0:T(8,128)(2,1)S(1)}, u32[]{:S(2)}, u32[]{:S(2)}) collective-permute-start(bf16[1,8,8,512]{3,2,1,0:T(8,128)(2,1)S(1)} %get-tuple-element.44), channel_id=1, source_target_pairs={{0,16},{16,32},{32,48},{48,64},{64,80},{80,96},{96,112},{112,128},... | collective-permute-start | bytes 196616 | tf_op jit(solution)/shard_map/ppermute | solution.py:371
  175.6 18.7 %collective-permute-start.3 = (bf16[1,8,8,512]{3,2,1,0:T(8,128)(2,1)S(1)}, bf16[1,8,8,512]{3,2,1,0:T(8,128)(2,1)S(1)}, u32[]{:S(2)}, u32[]{:S(2)}) collective-permute-start(bf16[1,8,8,512]{3,2,1,0:T(8,128)(2,1)S(1)} %get-tuple-element.45), channel_id=1, source_target_pairs={{16,0},{32,16},{48,32},{64,48},{80,64},{96,80},{112,96},{128,112},... | collective-permute-start | bytes 196616 | tf_op jit(solution)/shard_map/ppermute | solution.py:372
  177.9 28.1 %all-to-all-start = ((bf16[16,3,3,3,512]{4,3,2,1,0:T(4,128)(2,1)}), bf16[16,3,3,3,512]{4,3,2,1,0:T(4,128)(2,1)S(1)}, u32[]{:S(2)}, u32[]{:S(2)}) async-start(bf16[16,3,3,3,512]{4,3,2,1,0:T(4,128)(2,1)} %broadcast_in_dim.2), calls=%async_computation | async-start | bytes 1179648 | tf_op jit(solution)/shard_map/all_to_all | solution.py:379

commit v2 on v1

v2 whole, which is shorter than its diff:
```python
import jax
import jax.numpy as jnp
from jax import lax
from jax.experimental import pallas as pl
from jax.experimental.pallas import tpu as pltpu
from jax.sharding import PartitionSpec as P

MESH = pl.DeviceIdType.MESH
BF = jnp.bfloat16
F32 = jnp.float32
DMA = pltpu.SemaphoreType.DMA


class Sends:
    def __init__(self, sems):
        self.sems, self.made = sems, []

    def go(self, src, dst, recv, device):
        copy = pltpu.make_async_remote_copy(
            src_ref=src,
            dst_ref=dst,
            send_sem=self.sems.at[len(self.made)],
            recv_sem=recv,
            device_id=device,
            device_id_type=MESH,
        )
        copy.start()
        self.made.append(copy)

    def finish(self):
        for copy in self.made:
            copy.wait_send()

    def arrived(self, dst, recv, device):
        pltpu.make_async_remote_copy(
            src_ref=dst,
            dst_ref=dst,
            send_sem=self.sems.at[0],
            recv_sem=recv,
            device_id=device,
            device_id_type=MESH,
        ).wait_recv()


class Place:
    def __init__(self):
        r, c = lax.axis_index("row"), lax.axis_index("col")
        self.r, self.c = r, c
        self.z, self.h = r // 2, r % 2
        self.x, self.l, self.k = c // 4, (c // 2) % 2, c % 2
        self.zp, self.zm = ((r + 2) % 16, c), ((r + 14) % 16, c)
        self.hp = (r + 1 - 2 * self.h, c)
        self.after, self.before = ((r + 1) % 16, c), ((r + 15) % 16, c)
        self.xp, self.xm = (r, (c + 4) % 16), (r, (c + 12) % 16)
        self.lp = (r, c + 2 - 4 * self.l)
        self.kp = (r, c + 1 - 2 * self.k)

    def slab(self, dz, other):
        hh = self.h + other * (1 - 2 * self.h)
        return ((self.z + dz + 8) % 8) * 2 + hh

    def tile(self, dx, other, k=None):
        ll = self.l + other * (1 - 2 * self.l)
        return ((self.x + dx + 4) % 4) * 4 + ll * 2 + (self.k if k is None else k)


class RowGather:
    def __init__(self, at, sends, buf, recv):
        self.at, self.sends, self.buf, self.recv = at, sends, buf, recv

    def start(self, own):
        at = self.at
        for peer, way in ((at.hp, 0), (at.zp, 0), (at.zm, 1)):
            self.sends.go(own, self.buf.at[at.r], self.recv.at[way, at.r], peer)

    def wait(self, j, way, rows=None):
        ref = self.buf.at[j] if rows is None else self.buf.at[j, pl.ds(rows, 64)]
        self.sends.arrived(ref, self.recv.at[way, j], self.at.hp)

    def pair(self):
        at = self.at
        j = at.slab(0, 1)
        self.wait(j, 0)
        for peer, way in ((at.zp, 0), (at.zm, 1)):
            self.sends.go(self.buf.at[j], self.buf.at[j], self.recv.at[way, j], peer)
        return [j]

    def step(self, s, other):
        at = self.at
        if s == 4:
            j = at.slab(4, other)
            self.wait(j, 0, 0)
            self.wait(j, 1, 64)
            return [j]
        got = []
        for way, dz, peer in ((0, -s, at.zp), (1, s, at.zm)):
            j = at.slab(dz, other)
            self.wait(j, way)
            ref = self.buf.at[j] if s < 3 else self.buf.at[j, pl.ds(64 * way, 64)]
            self.sends.go(ref, ref, self.recv.at[way, j], peer)
            got.append(j)
        return got


class ColGather:
    def __init__(self, at, sends, buf, recv):
        self.at, self.sends, self.buf, self.recv = at, sends, buf, recv

    def start(self, own):
        at = self.at
        for peer, way in ((at.lp, 0), (at.xp, 0), (at.xm, 1), (at.kp, 0)):
            self.sends.go(own, self.buf.at[at.c], self.recv.at[way, at.c], peer)

    def wait(self, j, way, rows=None):
        ref = self.buf.at[j] if rows is None else self.buf.at[j, pl.ds(rows, 64)]
        self.sends.arrived(ref, self.recv.at[way, j], self.at.kp)

    def pair(self):
        at = self.at
        j = at.tile(0, 1)
        self.wait(j, 0)
        for peer, way in ((at.xp, 0), (at.xm, 1), (at.kp, 0)):
            self.sends.go(self.buf.at[j], self.buf.at[j], self.recv.at[way, j], peer)

    def step(self, s, other):
        at = self.at
        if s == 2:
            j = at.tile(2, other)
            self.wait(j, 0, 0)
            self.wait(j, 1, 64)
            self.sends.go(self.buf.at[j], self.buf.at[j], self.recv.at[0, j], at.kp)
            return
        for way, dx, peer in ((0, -1, at.xp), (1, 1, at.xm)):
            j = at.tile(dx, other)
            self.wait(j, way)
            ref = self.buf.at[j, pl.ds(64 * way, 64)]
            self.sends.go(ref, ref, self.recv.at[way, j], peer)
            self.sends.go(self.buf.at[j], self.buf.at[j], self.recv.at[0, j], at.kp)

    def rest(self):
        for dx, other in ((0, 0), (0, 1), (1, 0), (1, 1), (-1, 0), (-1, 1), (2, 0), (2, 1)):
            self.wait(self.at.tile(dx, other, 1 - self.at.k), 0)


def shifts(line):
    at = lax.broadcasted_iota(jnp.int32, line.shape, 0)
    zero = jnp.zeros_like(line)
    return (
        jnp.where(at == 0, zero, pltpu.roll(line, 1, 0)),
        line,
        jnp.where(at == 7, zero, pltpu.roll(line, 7, 0)),
    )


def clear_rim(frame):
    zero = jnp.zeros(frame.shape[3:], F32)
    for e in range(3):
        for plane in range(4):
            frame[e, plane, 0] = zero
            frame[e, plane, 9] = zero


def fill_plane(frame, plane, read):
    def two(i, carry):
        rows = read(i)
        for half in range(2):
            for e, line in enumerate(shifts(rows[8 * half : 8 * half + 8])):
                frame[e, plane, 2 * i + half + 1] = line
        return carry

    lax.fori_loop(0, 4, two, 0)


def convolve(frame, taps, flipped, base, write):
    def line(i, carry):
        for half in range(2):
            y = 2 * i + half
            plane, y = y // 8, y % 8
            total = frame[1, plane + 1, y + 1]
            for a in range(3):
                for b in range(3):
                    for e in range(3):
                        tap = taps[2 - a, 2 - b, 2 - e] if flipped else taps[a, b, e]
                        total = total + tap * frame[e, plane + a, y + b]
            base[8 * half : 8 * half + 8] = total
        write(i, base[...])
        return carry

    lax.fori_loop(0, 8, line, 0)


def tap_totals(grads, frame, store):
    for lanes in range(0, grads.shape[1], 128):
        cut = pl.ds(lanes, 128)

        def line(i, totals):
            plane, y = i // 8, i % 8
            grad = grads[pl.ds(pl.multiple_of(i * 8, 8), 8), cut]
            return tuple(
                totals[9 * a + 3 * b + e] + grad * frame[e, plane + a, y + b, :, cut]
                for a in range(3)
                for b in range(3)
                for e in range(3)
            )

        totals = lax.fori_loop(0, 16, line, tuple(jnp.zeros((8, 128), F32) for _ in range(27)))
        for n, total in enumerate(totals):
            store(n, cut, jnp.sum(total, axis=0, keepdims=True))


def rowwise(n, work):
    def some(i, carry):
        work(pl.ds(pl.multiple_of(i * 32, 32), 32))
        return carry

    lax.fori_loop(0, n // 32, some, 0)


def flat(value):
    return value.reshape(value.shape[0] * value.shape[1], value.shape[2])


def rows_dot(a, b):
    return lax.dot_general(a, b, (((0,), (0,)), ((), ())), preferred_element_type=F32)


def whole(
    px, og, taps, gate, up, wg, wu, wd,
    pgrad, kgrad, gw, uw, dw,
    dy_all, x_all, g_all, u_all, dh_all, hid, ga, ub,
    wdt, wgt, wut, part, mate, stage, xp_half, xm_half, xp_full, xm_full, y_full,
    rstage, rhalf, rfull, rpair,
    px_rim, gr_rim, gr_out, frame, gframe, lines, total, tap_out, tap_in, tap_all,
    send_sem, dy_sem, x_sem, g_sem, u_sem, dh_sem, mate_sem, ring_sem, rring_sem, rim_sem, tap_sem,
):
    at = Place()
    sends = Sends(send_sem)
    barrier = pltpu.get_barrier_semaphore()
    row_peers = [((at.r + d) % 16, at.c) for d in range(1, 16)]
    peers = row_peers + [at.xp, at.xm, at.lp, at.kp]
    for peer in peers:
        pl.semaphore_signal(barrier, inc=1, device_id=peer, device_id_type=MESH)
    wdt[...] = wd[...].T
    dy_all[at.r] = og[...]
    g_all[at.c] = gate[...]
    u_all[at.c] = up[...]
    pl.semaphore_wait(barrier, len(peers))

    dy = RowGather(at, sends, dy_all, dy_sem)
    xg = RowGather(at, sends, x_all, x_sem)
    gg = ColGather(at, sends, g_all, g_sem)
    ug = ColGather(at, sends, u_all, u_sem)
    dg = ColGather(at, sends, dh_all, dh_sem)
    dy.start(og)
    sends.go(px.at[pl.ds(64, 64)], px_rim.at[0], rim_sem.at[0], at.after)
    sends.go(px.at[pl.ds(0, 64)], px_rim.at[1], rim_sem.at[1], at.before)
    gg.start(gate)
    ug.start(up)

    def partial(j):
        part[j] = jnp.dot(dy_all[j], wdt[...], preferred_element_type=F32).astype(BF)

    def to_mate(zz):
        j = zz * 2 + 1 - at.k
        sends.go(part.at[j], mate.at[zz], mate_sem.at[zz], at.kp)

    def zed(dz):
        return (at.z + dz + 8) % 8

    def rims(rim, sem, inside):
        for side, (peer, end) in enumerate(((at.before, 0), (at.after, 15))):
            sends.arrived(rim.at[side], sem.at[side], peer)
            fill_plane(
                inside,
                3 * side,
                lambda i: jnp.where(
                    at.r == end, 0.0, rim[side, pl.ds(pl.multiple_of(i * 16, 16), 16)].astype(F32)
                ),
            )

    partial(at.r)
    clear_rim(frame)
    clear_rim(gframe)
    for plane in (0, 1):
        fill_plane(
            frame,
            plane + 1,
            lambda i: px[pl.ds(pl.multiple_of(plane * 64 + i * 16, 16), 16)].astype(F32),
        )
    for j in dy.pair():
        partial(j)
    to_mate(at.z)
    gg.pair()
    ug.pair()
    for s in (1, 2, 3):
        for other in (0, 1):
            for j in dy.step(s, other):
                partial(j)
            if s == 1:
                gg.step(1, other)
            elif s == 2:
                gg.step(2, other)
            else:
                ug.step(1, other)
        to_mate(zed(s))
        to_mate(zed(-s))
        if s == 1:
            rims(px_rim, rim_sem, frame)

            def mixed(i, value):
                x_all[at.r, pl.ds(pl.multiple_of(i * 16, 16), 16)] = value.astype(BF)

            convolve(frame, taps, False, lines, mixed)
    xg.start(x_all.at[at.r])
    for other in (0, 1):
        for j in dy.step(4, other):
            partial(j)
    to_mate(zed(4))
    for other in (0, 1):
        ug.step(2, other)
    xg.pair()

    def ell(other):
        return at.l + other * (1 - 2 * at.l)

    def summed(xx, ll, rows):
        zz = xx * 2 + ll
        return part[zz * 2 + at.k, rows].astype(F32) + mate[zz, rows].astype(F32)

    def from_mate(xx, ll):
        zz = xx * 2 + ll
        sends.arrived(mate.at[zz], mate_sem.at[zz], at.kp)

    def ex(dx):
        return (at.x + dx + 4) % 4

    for o in (1, 0):
        ll, xx = ell(o), ex(2)
        from_mate(xx, ll)

        def far(rows):
            stage[0, o, rows] = summed(xx, ll, rows).astype(BF)

        rowwise(128, far)
        sends.go(stage.at[0, o, pl.ds(0, 64)], xp_half.at[ll], ring_sem.at[0, ll], at.xp)
        sends.go(stage.at[0, o, pl.ds(64, 64)], xm_half.at[ll], ring_sem.at[1, ll], at.xm)
    for other in (0, 1):
        xg.step(1, other)
    gg.rest()
    ug.rest()

    def swiglu(j):
        def work(rows):
            g, u = g_all[j, rows].astype(F32), u_all[j, rows].astype(F32)
            s = 1.0 / (1.0 + jnp.exp(-g))
            silu = g * s
            hid[j, rows] = (silu * u).astype(BF)
            ga[j, rows] = (u * (s + silu * (1.0 - s))).astype(BF)
            ub[j, rows] = silu.astype(BF)

        rowwise(128, work)

    def swiglus(lo, hi):
        lax.fori_loop(lo, hi, lambda j, carry: (swiglu(j), carry)[1], 0)

    swiglus(0, 4)
    for o in (1, 0):
        ll = ell(o)
        for way, half, full, peer, source in (
            (0, xp_half, xp_full, at.xp, at.xm),
            (1, xm_half, xm_full, at.xm, at.xp),
        ):
            xx = ex(1 - 2 * way)
            from_mate(xx, ll)
            sends.arrived(half.at[ll], ring_sem.at[way, ll], source)

            def near(i, carry):
                rows = pl.ds(pl.multiple_of(64 * way + i * 32, 32), 32)
                came = half[ll, pl.ds(pl.multiple_of(i * 32, 32), 32)].astype(F32)
                stage[1 + way, o, rows] = (summed(xx, ll, rows) + came).astype(BF)
                rows = pl.ds(pl.multiple_of(64 - 64 * way + i * 32, 32), 32)
                stage[1 + way, o, rows] = summed(xx, ll, rows).astype(BF)
                return carry

            lax.fori_loop(0, 2, near, 0)
            sends.go(stage.at[1 + way, o], full.at[ll], ring_sem.at[2 + way, ll], peer)
    swiglus(4, 10)
    for other in (0, 1):
        xg.step(2, other)

    for o in (1, 0):
        ll = ell(o)
        from_mate(at.x, ll)
        sends.arrived(xp_full.at[ll], ring_sem.at[2, ll], at.xm)
        sends.arrived(xm_full.at[ll], ring_sem.at[3, ll], at.xp)
        if o == 0:
            sends.arrived(y_full, ring_sem.at[4, 0], at.lp)

        def last(rows):
            value = summed(at.x, ll, rows) + xp_full[ll, rows].astype(F32)
            value = value + xm_full[ll, rows].astype(F32)
            if o == 1:
                stage[3, 0, rows] = value.astype(BF)
            else:
                dh_all[at.c, rows] = (value + y_full[rows].astype(F32)).astype(BF)

        rowwise(128, last)
        if o == 1:
            sends.go(stage.at[3, 0], y_full, ring_sem.at[4, 0], at.lp)
    dg.start(dh_all.at[at.c])
    swiglus(10, 16)
    dg.pair()
    for other in (0, 1):
        xg.step(3, other)

    def down(lo, n):
        lhs = flat(hid[:, :, lo : lo + n])
        dw[lo : lo + n, :] = rows_dot(lhs, flat(dy_all[...])).astype(BF)

    down(0, 256)
    for other in (0, 1):
        dg.step(1, other)
    wgt[...] = wg[...].T
    wut[...] = wu[...].T
    down(256, 256)
    for other in (0, 1):
        xg.step(4, other)
    for other in (0, 1):
        dg.step(2, other)
    dg.rest()

    def hidden_grads(j):
        def work(rows):
            grad = dh_all[j, rows].astype(F32)
            ga[j, rows] = (ga[j, rows].astype(F32) * grad).astype(BF)
            ub[j, rows] = (ub[j, rows].astype(F32) * grad).astype(BF)

        rowwise(128, work)

    def back(j):
        return jnp.dot(ga[j], wgt[...], preferred_element_type=F32) + jnp.dot(
            ub[j], wut[...], preferred_element_type=F32
        )

    for other in (1, 0):
        j = at.slab(4, other)
        hidden_grads(j)
        total[...] = back(j)
        for way, peer in ((0, at.zp), (1, at.zm)):
            rows = pl.ds(64 * way, 64)
            rstage[0, way, other, rows] = total[rows].astype(BF)
            sends.go(
                rstage.at[0, way, other, rows],
                rhalf.at[way, other],
                rring_sem.at[0, way, other],
                peer,
            )

    def rest_of_hidden(n, carry):
        hidden_grads((at.z * 2 + 10 + n) % 16)
        return carry

    lax.fori_loop(0, 14, rest_of_hidden, 0)

    def wgrad(out, right, lo):
        out[lo : lo + 256, :] = rows_dot(flat(x_all[:, :, lo : lo + 256]), flat(right[...])).astype(BF)

    for t in (1, 2, 3):
        for other in (1, 0):
            for way, peer, source in ((0, at.zp, at.zm), (1, at.zm, at.zp)):
                j = at.slab((4 - t) * (1 - 2 * way), other)
                total[...] = back(j)
                if t == 1:
                    sends.arrived(rhalf.at[way, other], rring_sem.at[0, way, other], source)
                    rows = pl.ds(64 * way, 64)
                    total[rows] = total[rows] + rhalf[way, other].astype(F32)
                else:
                    sends.arrived(rfull.at[t - 2, way, other], rring_sem.at[t - 1, way, other], source)
                    total[...] = total[...] + rfull[t - 2, way, other].astype(F32)
                rstage[t, way, other] = total[...].astype(BF)
                sends.go(
                    rstage.at[t, way, other],
                    rfull.at[t - 1, way, other],
                    rring_sem.at[t, way, other],
                    peer,
                )
        if t == 1:
            wgrad(gw, ga, 0)
        elif t == 2:
            wgrad(gw, ga, 256)
            down(512, 256)
        else:
            wgrad(uw, ub, 0)
    for other in (1, 0):
        j = at.slab(0, other)
        total[...] = back(j)
        for way, source in ((0, at.zm), (1, at.zp)):
            sends.arrived(rfull.at[2, way, other], rring_sem.at[3, way, other], source)
            total[...] = total[...] + rfull[2, way, other].astype(F32)
        if other == 1:
            rpair[0] = total[...].astype(BF)
            sends.go(rpair.at[0], rpair.at[1], rring_sem.at[4, 0, 0], at.hp)
    total[...] = total[...] + og[...].astype(F32)
    sends.arrived(rpair.at[1], rring_sem.at[4, 0, 0], at.hp)
    total[...] = total[...] + rpair[1].astype(F32)

    gr_out[...] = total[...].astype(BF)
    sends.go(gr_out.at[pl.ds(64, 64)], gr_rim.at[0], rim_sem.at[2], at.after)
    sends.go(gr_out.at[pl.ds(0, 64)], gr_rim.at[1], rim_sem.at[3], at.before)

    def tap_store(n, cut, value):
        tap_out[n // 2, n % 2 : n % 2 + 1, cut] = value

    tap_totals(total, frame, tap_store)
    tap_out[13, 1:2] = jnp.zeros((1, tap_out.shape[2]), F32)
    tap_out[14] = jnp.zeros(tap_out.shape[1:], F32)
    tap_out[15] = jnp.zeros(tap_out.shape[1:], F32)
    for n, peer in enumerate(row_peers):
        j = (at.r + n + 1) % 16
        sends.go(tap_out.at[j], tap_in.at[at.r], tap_sem.at[0, at.r], peer)
    for plane in (0, 1):
        fill_plane(
            gframe,
            plane + 1,
            lambda i: total[pl.ds(pl.multiple_of(plane * 64 + i * 16, 16), 16)],
        )
    wgrad(uw, ub, 256)
    down(768, 128)
    tap_in[at.r] = tap_out[at.r]
    for n, peer in enumerate(row_peers):
        j = (at.r + n + 1) % 16
        sends.arrived(tap_in.at[j], tap_sem.at[0, j], peer)
    tap_all[at.r] = jnp.sum(tap_in[...], axis=0)
    for n, peer in enumerate(row_peers):
        sends.go(tap_all.at[at.r], tap_all.at[at.r], tap_sem.at[1, at.r], peer)
    rims(gr_rim, rim_sem.at[pl.ds(2, 2)], gframe)

    def grads(i, value):
        pgrad[pl.ds(pl.multiple_of(i * 16, 16), 16)] = value.astype(BF)

    convolve(gframe, taps, True, lines, grads)
    for n, peer in enumerate(row_peers):
        j = (at.r + n + 1) % 16
        sends.arrived(tap_all.at[j], tap_sem.at[1, j], peer)
    for n in range(27):
        kgrad[n] = tap_all[n // 2, n % 2 : n % 2 + 1]
    sends.finish()


VM = pl.BlockSpec(memory_space=pltpu.VMEM)


def run(px, og, taps, gate, up, wg, wu, wd):
    feats, units = og.shape[1], gate.shape[1]
    tok, hid = (16, 128, feats), (16, 128, units)
    vm = pltpu.VMEM
    return pl.pallas_call(
        whole,
        out_shape=[
            jax.ShapeDtypeStruct((128, feats), BF),
            jax.ShapeDtypeStruct((27, 1, feats), F32),
            jax.ShapeDtypeStruct((feats, units), BF),
            jax.ShapeDtypeStruct((feats, units), BF),
            jax.ShapeDtypeStruct((units, feats), BF),
        ],
        in_specs=[VM] * 8,
        out_specs=[VM] * 5,
        scratch_shapes=[
            *(vm(s, BF) for s in (tok, tok, hid, hid, hid, hid, hid, hid)),
            vm((feats, units), BF),
            vm((units, feats), BF),
            vm((units, feats), BF),
            vm(hid, BF),
            vm((8, 128, units), BF),
            vm((4, 2, 128, units), BF),
            vm((2, 64, units), BF),
            vm((2, 64, units), BF),
            vm((2, 128, units), BF),
            vm((2, 128, units), BF),
            vm((128, units), BF),
            vm((4, 2, 2, 128, feats), BF),
            vm((2, 2, 64, feats), BF),
            vm((3, 2, 2, 128, feats), BF),
            vm((2, 128, feats), BF),
            vm((2, 64, feats), BF),
            vm((2, 64, feats), BF),
            vm((128, feats), BF),
            vm((3, 4, 10, 8, feats), F32),
            vm((3, 4, 10, 8, feats), F32),
            vm((16, feats), F32),
            vm((128, feats), F32),
            vm((16, 2, feats), F32),
            vm((16, 2, feats), F32),
            vm((16, 2, feats), F32),
            DMA((170,)),
            DMA((2, 16)),
            DMA((2, 16)),
            DMA((2, 16)),
            DMA((2, 16)),
            DMA((2, 16)),
            DMA((8,)),
            DMA((5, 2)),
            DMA((5, 2, 2)),
            DMA((4,)),
            DMA((2, 16)),
        ],
        compiler_params=pltpu.CompilerParams(
            collective_id=0, has_side_effects=True, vmem_limit_bytes=67043328
        ),
        name="whole",
    )(px, og, taps, gate, up, wg, wu, wd)


def body(patches, out_grad, conv_kernel, saved_gate, saved_up, w_gate, w_up, w_down):
    planes, height, breadth, features = patches.shape
    own = planes * height * breadth
    patch_grad, kernel_grad, gate_wgrad, up_wgrad, down_wgrad = run(
        patches.reshape(own, features),
        out_grad.reshape(own, features),
        conv_kernel.reshape(3, 3, 3, 1, features),
        saved_gate,
        saved_up,
        w_gate,
        w_up,
        w_down,
    )
    return (
        patch_grad.reshape(patches.shape),
        kernel_grad.reshape(conv_kernel.shape),
        gate_wgrad,
        up_wgrad,
        down_wgrad,
    )


def solution(mesh):
    return jax.shard_map(
        body,
        mesh=mesh,
        in_specs=(
            P("row", None, None, "col"),
            P("row", None, None, "col"),
            P(None, None, None, "col"),
            P("col", "row"),
            P("col", "row"),
            P("col", "row"),
            P("col", "row"),
            P("row", "col"),
        ),
        out_specs=(
            P("row", None, None, "col"),
            P(None, None, None, "col"),
            P("col", "row"),
            P("col", "row"),
            P("row", "col"),
        ),
        check_vma=False,
    )
```

time: 207 us -> 143 us (0.69)
  matrix products: 25.6 us -> 0 us
  starting transfers between devices: 20.7 us -> 0 us
  waiting for transfers between devices: 14.9 us -> 0 us
  other arithmetic: 14.9 us -> 0.98 us
  Pallas kernels: 125 us -> 133 us
  local copies, waits for them, and re-layouts: 4.74 us -> 7.55 us
    dot_general x5 -> x0, matrix products: 25.6 us -> none  [the longest x1 7.31 us: body(): lax.dot_general(flat_in, up_grad_all, contract_rows, preferred_element_ty...]
    ppermute x4 -> x0, starting transfers between devices: 11.5 us -> none  [the longest x2 8.91 us: padded(): before = lax.ppermute(last, axis, up)]
    convert_element_type x6 -> x0, other arithmetic: 11.5 us -> none  [the longest x1 6.77 us: swiglu_back(): up_grad = (hidden_grad * silu_g).astype(jnp.bfloat16)]
    all_to_all x1 -> x0, waiting for transfers between devices: 10.3 us -> none  [from_everyone(): lax.all_to_all(jnp.broadcast_to(x[None], (peers, *x.shape)), axis, 0, 0,...]
    all_to_all x1 -> x0, starting transfers between devices: 9.16 us -> none  [from_everyone(): lax.all_to_all(jnp.broadcast_to(x[None], (peers, *x.shape)), axis, 0, 0,...]
    pallas_call x2 -> x1, Pallas kernels: 125 us -> 133 us  [run(): pl.pallas_call(whole, out_shape=[jax.ShapeDtypeStruct((128, feats), BF),...]
    ppermute x4 -> x0, waiting for transfers between devices: 4.6 us -> none  [the longest x2 4.59 us: padded(): after = lax.ppermute(first, axis, down)]
    unnamed x14 -> x10, local copies, waits for them, and re-layouts: 0.75 us -> 5.35 us
  transfers between devices with their start and end apart: 5 -> 0, of which waited for: 2 -> 0; matrix products, arithmetic and copies ran while one was open for 5% -> 0% of each run, Pallas kernels for 0% -> 0%
where the time goes in v2:
time: 143 us; the launch traced here: 142 us
  Pallas kernels  133 us (93%)
  local copies, waits for them, and re-layouts  7.55 us (5%)
    pallas_call x1, Pallas kernels, run(): pl.pallas_call(whole, out_shape=[jax.ShapeDtypeStruct((128, feats), BF),...  133 us
    unnamed x10, local copies, waits for them, and re-layouts  5.35 us

profile of v2, /device:TPU:2, one launch (start us, length us, event | category | flops | bytes accessed | tf_op | source)
XLA Modules:
  0.0 142.3 jit_solution(8099157170752956000)
XLA Ops:
  0.6 1.5 %reshape.27.taps = f32[3,3,3,1,512]{4,3,2,1,0:T(1,128)} reshape(f32[3,3,3,512]{3,2,1,0:T(4,128)} %param.10) | data formatting | bytes 110592 | tf_op jit(solution)/shard_map/reshape | solution.py:620
  2.2 133.1 %whole.1 = (bf16[128,512]{1,0:T(8,128)(2,1)}, f32[27,1,512]{2,1,0:T(1,128)}, bf16[512,896]{1,0:T(8,128)(2,1)}, bf16[512,896]{1,0:T(8,128)(2,1)}, bf16[896,512]{1,0:T(8,128)(2,1)}) custom-call(bf16[128,512]{1,0:T(8,128)(2,1)} %bitcast.4, bf16[128,512]{1,0:T(8,128)(2,1)} %bitcast.5, f32[3,3,3,1,512]{4,3,2,1,0:T(1,128)} %reshape.27.taps, ...), custom_call_target="tpu_custom_call" | custom-call | tf_op jit(solution)/shard_map/whole/pallas_call | solution.py:557
  135.3 0.0 copy-start.2
  135.3 1.0 reduce
  136.3 0.7 reshape.29
  137.0 0.0 copy-done.2
  137.0 0.7 copy.18
  137.6 0.0 copy-start.1
  137.6 2.3 %copy.19 = bf16[512,896]{1,0:T(8,128)(2,1)} copy(bf16[512,896]{1,0:T(8,128)(2,1)} %get-tuple-element.22) | data formatting | bytes 1835008
  139.9 0.0 copy-done.1
  139.9 0.0 copy-start
  139.9 0.9 copy.20
  140.8 0.6 copy-done
  141.4 0.9 copy.21
Async XLA Ops:
  135.3 1.7 %copy-start.2 = (bf16[128,512]{1,0:T(8,128)(2,1)S(1)}, bf16[128,512]{1,0:T(8,128)(2,1)}, u32[]{:S(2)}) copy-start(bf16[128,512]{1,0:T(8,128)(2,1)} %get-tuple-element.10) | copy-start | bytes 393220
  137.6 2.3 %copy-start.1 = (bf16[512,896]{1,0:T(8,128)(2,1)S(1)}, bf16[512,896]{1,0:T(8,128)(2,1)}, u32[]{:S(2)}) copy-start(bf16[512,896]{1,0:T(8,128)(2,1)} %get-tuple-element.23) | copy-start | bytes 2752516
  139.9 1.5 %copy-start = (bf16[896,512]{1,0:T(8,128)(2,1)S(1)}, bf16[896,512]{1,0:T(8,128)(2,1)}, u32[]{:S(2)}) copy-start(bf16[896,512]{1,0:T(8,128)(2,1)} %get-tuple-element.24) | copy-start | bytes 2752516

commit v3 on v0

v3 whole, which is shorter than its diff:
```python
import jax
import jax.numpy as jnp
from jax import lax
from jax.experimental import pallas as pl
from jax.experimental.pallas import tpu as pltpu
from jax.sharding import PartitionSpec as P

MESH = pl.DeviceIdType.MESH
BF = jnp.bfloat16
F32 = jnp.float32
DMA = pltpu.SemaphoreType.DMA


class Sends:
    def __init__(self, sem):
        self.sem = sem

    def copy(self, src, dst, recv, device):
        return pltpu.make_async_remote_copy(
            src_ref=src,
            dst_ref=dst,
            send_sem=self.sem,
            recv_sem=recv,
            device_id=device,
            device_id_type=MESH,
        )

    def go(self, src, dst, recv, device):
        self.copy(src, dst, recv, device).start()

    def arrived(self, dst, recv, device):
        self.copy(dst, dst, recv, device).wait_recv()

    def finish(self, as_large, recv, device):
        self.copy(as_large, as_large, recv, device).wait_send()


class Place:
    def __init__(self):
        r, c = lax.axis_index("row"), lax.axis_index("col")
        self.r, self.c = r, c
        self.z, self.h = r // 2, r % 2
        self.x, self.l, self.k = c // 4, (c // 2) % 2, c % 2
        self.zp, self.zm = ((r + 2) % 16, c), ((r + 14) % 16, c)
        self.hp = (r + 1 - 2 * self.h, c)
        self.after, self.before = ((r + 1) % 16, c), ((r + 15) % 16, c)
        self.xp, self.xm = (r, (c + 4) % 16), (r, (c + 12) % 16)
        self.lp = (r, c + 2 - 4 * self.l)
        self.kp = (r, c + 1 - 2 * self.k)

    def slab(self, dz, other):
        hh = self.h + other * (1 - 2 * self.h)
        return ((self.z + dz + 8) % 8) * 2 + hh

    def tile(self, dx, other):
        return (self.x + dx + 4) % 4, self.l + other * (1 - 2 * self.l), self.k

    def number(self, t):
        return t[0] * 4 + t[1] * 2 + t[2]


class RowGather:
    def __init__(self, at, sends, buf, recv, base, n):
        self.at, self.sends, self.buf, self.recv, self.base, self.n = at, sends, buf, recv, base, n

    def ref(self, j, lo=0, size=None):
        return self.buf.at[j, pl.ds(self.base + lo, self.n if size is None else size)]

    def sem(self, way, s, other):
        return self.recv.at[8 * way + 2 * (s - 1) + other]

    def start(self, own):
        at, ref = self.at, self.ref(self.at.r)
        self.sends.go(own, ref, self.recv.at[16], at.hp)
        self.sends.go(own, ref, self.sem(0, 1, 0), at.zp)
        self.sends.go(own, ref, self.sem(1, 1, 0), at.zm)

    def wait(self, j, sem, lo=0, size=None):
        self.sends.arrived(self.ref(j, lo, size), sem, self.at.hp)

    def pair(self):
        at = self.at
        j = at.slab(0, 1)
        self.wait(j, self.recv.at[16])
        for peer, way in ((at.zp, 0), (at.zm, 1)):
            self.sends.go(self.ref(j), self.ref(j), self.sem(way, 1, 1), peer)
        return [j]

    def step(self, s):
        at, half, got = self.at, self.n // 2, []
        for other in (0, 1):
            if s == 4:
                j = at.slab(4, other)
                self.wait(j, self.sem(0, 4, other), 0, half)
                self.wait(j, self.sem(1, 4, other), half, half)
                got.append(j)
                continue
            for way, dz, peer in ((0, -s, at.zp), (1, s, at.zm)):
                j = at.slab(dz, other)
                self.wait(j, self.sem(way, s, other))
                ref = self.ref(j) if s < 3 else self.ref(j, half * way, half)
                self.sends.go(ref, ref, self.sem(way, s + 1, other), peer)
                got.append(j)
        return got

    def finish(self):
        sent = self.buf.at[pl.ds(0, 15), pl.ds(self.base, self.n)]
        self.sends.finish(sent, self.recv.at[16], self.at.hp)


class ColGather:
    def __init__(self, at, sends, buf, recv, base, n):
        self.at, self.sends, self.buf, self.recv, self.base, self.n = at, sends, buf, recv, base, n

    def ref(self, t, lo, size):
        return self.buf.at[self.at.number(t), pl.ds(self.base + lo, size)]

    def ring(self, way, s, other):
        return 4 * way + 2 * (s - 1) + other

    def move(self, t, sem, peer, lo=0, size=None, own=None):
        ref = self.ref(t, lo, self.n if size is None else size)
        self.sends.go(ref if own is None else own, ref, self.recv.at[sem], peer)

    def wait(self, t, sem, lo=0, size=None):
        ref = self.ref(t, lo, self.n if size is None else size)
        self.sends.arrived(ref, self.recv.at[sem], self.at.kp)

    def start(self, own=None):
        at, t = self.at, self.at.tile(0, 0)
        self.move(t, 12, at.lp, own=own)
        self.move(t, self.ring(0, 1, 0), at.xp, own=own)
        self.move(t, self.ring(1, 1, 0), at.xm, own=own)
        self.move(t, 11, at.kp, own=own)

    def pair(self):
        at, t, half = self.at, self.at.tile(0, 1), self.n // 2
        self.wait(t, 12)
        self.move(t, self.ring(0, 1, 1), at.xp, 0, half)
        self.move(t, self.ring(1, 1, 1), at.xm, 0, half)
        self.move(t, 11, at.kp)

    def step1(self):
        at, half, quarter = self.at, self.n // 2, self.n // 4
        for way, dx, peer in ((0, -1, at.xp), (1, 1, at.xm)):
            t = at.tile(dx, 0)
            self.wait(t, self.ring(way, 1, 0))
            self.move(t, self.ring(way, 2, 0), peer, half * way, half)
            self.move(t, 8 + way, at.lp, half, half)
            self.move(t, 11, at.kp)
        for way, dx, peer in ((0, -1, at.xp), (1, 1, at.xm)):
            t = at.tile(dx, 1)
            self.wait(t, self.ring(way, 1, 1), 0, half)
            self.move(t, self.ring(way, 2, 1), peer, quarter * way, quarter)

    def step2(self):
        at, half, quarter = self.at, self.n // 2, self.n // 4
        t = at.tile(2, 0)
        self.wait(t, self.ring(1, 2, 0), half, half)
        self.move(t, 10, at.lp, half, half)
        self.wait(t, self.ring(0, 2, 0), 0, half)
        self.move(t, 11, at.kp)
        for way, dx in ((0, -1), (1, 1)):
            t = at.tile(dx, 1)
            self.wait(t, 8 + way, half, half)
            self.move(t, 11, at.kp)
        t = at.tile(2, 1)
        self.wait(t, self.ring(0, 2, 1), 0, quarter)
        self.wait(t, self.ring(1, 2, 1), quarter, quarter)

    def step3(self):
        at, half = self.at, self.n // 2
        t = at.tile(2, 1)
        self.wait(t, 10, half, half)
        self.move(t, 11, at.kp)

    def many(self, tiles):
        return self.buf.at[pl.ds(0, tiles), pl.ds(self.base, self.n)]

    def rest(self):
        self.sends.arrived(self.many(8), self.recv.at[11], self.at.kp)

    def finish(self):
        self.sends.finish(self.many(15), self.recv.at[11], self.at.kp)


class ColReduce:
    def __init__(self, at, sends, mate_sends, base, part, mate, mate_sem, stage, halves, fulls, pair, sem, put):
        self.at, self.sends, self.mate_sends, self.base = at, sends, mate_sends, base
        self.part, self.mate, self.mate_sem = part, mate, mate_sem
        self.stage, self.halves, self.fulls, self.pair, self.sem, self.put = (
            stage, halves, fulls, pair, sem, put,
        )

    def ell(self, o):
        return self.at.l + o * (1 - 2 * self.at.l)

    def ex(self, dx):
        return (self.at.x + dx + 4) % 4

    def mated(self, dx, o):
        zz = self.ex(dx) * 2 + self.ell(o)
        self.mate_sends.arrived(
            self.mate.at[zz, pl.ds(self.base, 64)], self.mate_sem.at[zz], self.at.kp
        )
        return zz

    def summed(self, zz, lo, n):
        rows = pl.ds(self.base + lo, n)
        return self.part[2 * zz + self.at.k, rows].astype(F32) + self.mate[zz, rows].astype(F32)

    def stage1(self):
        at = self.at
        for o in (1, 0):
            ll = self.ell(o)
            j = self.mated(2, o)
            for lo in (0, 32):
                self.stage[0, o, lo : lo + 32] = self.summed(j, lo, 32).astype(BF)
            for way, peer in ((0, at.xp), (1, at.xm)):
                self.sends.go(
                    self.stage.at[0, o, pl.ds(32 * way, 32)],
                    self.halves.at[way, ll],
                    self.sem.at[way, ll],
                    peer,
                )

    def stage2(self):
        at = self.at
        for o in (1, 0):
            ll = self.ell(o)
            for way, peer, source in ((0, at.xp, at.xm), (1, at.xm, at.xp)):
                j = self.mated(1 - 2 * way, o)
                self.sends.arrived(self.halves.at[way, ll], self.sem.at[way, ll], source)
                lo = 32 * way
                self.stage[1 + way, o, lo : lo + 32] = (
                    self.summed(j, lo, 32) + self.halves[way, ll].astype(F32)
                ).astype(BF)
                lo = 32 - lo
                self.stage[1 + way, o, lo : lo + 32] = self.summed(j, lo, 32).astype(BF)
                self.sends.go(
                    self.stage.at[1 + way, o], self.fulls.at[way, ll], self.sem.at[2 + way, ll], peer
                )

    def full(self, o):
        at, ll = self.at, self.ell(o)
        j = self.mated(0, o)
        self.sends.arrived(self.fulls.at[0, ll], self.sem.at[2, ll], at.xm)
        self.sends.arrived(self.fulls.at[1, ll], self.sem.at[3, ll], at.xp)

        def value(lo):
            total = self.summed(j, lo, 32) + self.fulls[0, ll, lo : lo + 32].astype(F32)
            return total + self.fulls[1, ll, lo : lo + 32].astype(F32)

        return value

    def stage3(self):
        at = self.at
        value = self.full(1)
        for lo in (0, 32):
            self.stage[3, 0, lo : lo + 32] = value(lo).astype(BF)
        self.sends.go(self.stage.at[3, 0], self.pair, self.sem.at[4, 0], at.lp)

    def finish(self):
        rows = pl.ds(self.base, 64)
        self.sends.finish(self.part.at[pl.ds(0, 7), rows], self.sem.at[4, 0], self.at.lp)
        self.mate_sends.finish(self.mate.at[:, rows], self.mate_sem.at[0], self.at.kp)

    def stage4(self):
        value = self.full(0)
        self.sends.arrived(self.pair, self.sem.at[4, 0], self.at.lp)
        for lo in (0, 32):
            self.put(lo, (value(lo) + self.pair[lo : lo + 32].astype(F32)).astype(BF))


def shifts(line):
    at = lax.broadcasted_iota(jnp.int32, line.shape, 0)
    zero = jnp.zeros_like(line)
    return (
        jnp.where(at == 0, zero, pltpu.roll(line, 1, 0)),
        line,
        jnp.where(at == 7, zero, pltpu.roll(line, 7, 0)),
    )


def clear_rim(frame):
    zero = jnp.zeros(frame.shape[3:], F32)
    for e in range(3):
        for plane in range(4):
            frame[e, plane, 0] = zero
            frame[e, plane, 9] = zero


def fill_plane(frame, plane, read):
    def two(i, carry):
        rows = read(i)
        for half in range(2):
            for e, line in enumerate(shifts(rows[8 * half : 8 * half + 8])):
                frame[e, plane, 2 * i + half + 1] = line
        return carry

    lax.fori_loop(0, 4, two, 0)


def convolve(frame, taps, flipped, base, write):
    def line(i, carry):
        for half in range(2):
            y = 2 * i + half
            plane, y = y // 8, y % 8
            total = frame[1, plane + 1, y + 1]
            for a in range(3):
                for b in range(3):
                    for e in range(3):
                        ta, tb, te = (2 - a, 2 - b, 2 - e) if flipped else (a, b, e)
                        tap = taps[ta, tb, te : te + 1, :]
                        total = total + tap * frame[e, plane + a, y + b]
            base[8 * half : 8 * half + 8] = total
        write(i, base[...])
        return carry

    lax.fori_loop(0, 8, line, 0)


def tap_totals(grads, frame, plane, store):
    for lanes in range(0, grads.shape[1], 128):
        cut = pl.ds(lanes, 128)

        def line(i, totals):
            grad = grads[pl.ds(pl.multiple_of(plane * 64 + i * 8, 8), 8), cut]
            return tuple(
                totals[9 * a + 3 * b + e] + grad * frame[e, plane + a, i + b, :, cut]
                for a in range(3)
                for b in range(3)
                for e in range(3)
            )

        totals = lax.fori_loop(0, 8, line, tuple(jnp.zeros((8, 128), F32) for _ in range(27)))
        for n, total in enumerate(totals):
            store(n, cut, jnp.sum(total, axis=0, keepdims=True))


def rowwise(n, work):
    def some(i, carry):
        work(pl.ds(pl.multiple_of(i * 32, 32), 32))
        return carry

    lax.fori_loop(0, n // 32, some, 0)


def flat(value):
    return value.reshape(value.shape[0] * value.shape[1], value.shape[2])


def rows_dot(a, b):
    return lax.dot_general(a, b, (((0,), (0,)), ((), ())), preferred_element_type=F32)


def whole(
    px, og, taps, gate, up, wg, wu, wd,
    pgrad, kgrad, gw, uw, dw,
    dy_all, x_all, g_all, u_all, dh_all, hid, ga, ub,
    wdt, wgt, wut, part, mate, stage, halves, fulls, pairs,
    rstage, rhalf, rfull, rpair,
    px_rim, gr_rim, gr_out, frame, gframe, lines, total, tap_out, tap_in, tap_all,
    send_sem, dy_sem, x_sem, g_sem, u_sem, h_sem, mate_sem, ring_sem, rring_sem, rim_sem, tap_sem,
):
    at = Place()
    count = iter(range(send_sem.shape[0]))

    def stream():
        return Sends(send_sem.at[next(count)])

    rim_sends, first_taps, last_taps = stream(), stream(), stream()
    mate_sends, back_sends = [stream(), stream()], [stream(), stream()]
    barrier = pltpu.get_barrier_semaphore()
    row_peers = [((at.r + d) % 16, at.c) for d in range(1, 16)]
    peers = row_peers + [at.xp, at.xm, at.lp, at.kp]
    for peer in peers:
        pl.semaphore_signal(barrier, inc=1, device_id=peer, device_id_type=MESH)
    wdt[...] = wd[...].T
    dy_all[at.r] = og[...]
    g_all[at.c] = gate[...]
    u_all[at.c] = up[...]
    pl.semaphore_wait(barrier, len(peers))

    def reduce(q):
        def put(lo, value):
            dh_all[at.c, 64 * q + lo : 64 * q + lo + 32] = value

        return ColReduce(
            at, stream(), mate_sends[q], 64 * q, part, mate, mate_sem.at[q],
            stage.at[q], halves.at[q], fulls.at[q], pairs.at[q], ring_sem.at[q], put,
        )

    both = (0, 1)
    dy = [RowGather(at, stream(), dy_all, dy_sem.at[q], 64 * q, 64) for q in both]
    xg = RowGather(at, stream(), x_all, x_sem, 0, 128)
    gg = [ColGather(at, stream(), g_all, g_sem.at[q], 64 * q, 64) for q in both]
    ug = [ColGather(at, stream(), u_all, u_sem.at[q], 64 * q, 64) for q in both]
    hg = [ColGather(at, stream(), dh_all, h_sem.at[q], 64 * q, 64) for q in both]
    red = [reduce(q) for q in both]

    def chunk(ref, q):
        return ref.at[pl.ds(64 * q, 64)]

    def partials(q, slabs):
        rows = pl.ds(64 * q, 64)
        for j in slabs:
            part[j, rows] = jnp.dot(
                dy_all[j, rows], wdt[...], preferred_element_type=F32
            ).astype(BF)

    def to_mate(q, dz):
        zz = (at.z + dz + 8) % 8
        rows = pl.ds(64 * q, 64)
        mate_sends[q].go(
            part.at[2 * zz + 1 - at.k, rows], mate.at[zz, rows], mate_sem.at[q, zz], at.kp
        )

    def dy_step(q, s):
        partials(q, dy[q].step(s))
        to_mate(q, s)
        if s < 4:
            to_mate(q, -s)

    def rims(rim, sem, inside):
        for side, (peer, end) in enumerate(((at.before, 0), (at.after, 15))):
            rim_sends.arrived(rim.at[side], sem.at[side], peer)
            fill_plane(
                inside,
                3 * side,
                lambda i: jnp.where(
                    at.r == end, 0.0, rim[side, pl.ds(pl.multiple_of(i * 16, 16), 16)].astype(F32)
                ),
            )

    def swiglu(q):
        def work(i, carry):
            j, rows = i // 2, pl.ds(pl.multiple_of(64 * q + i % 2 * 32, 32), 32)
            g, u = g_all[j, rows].astype(F32), u_all[j, rows].astype(F32)
            s = 1.0 / (1.0 + jnp.exp(-g))
            silu = g * s
            hid[j, rows] = (silu * u).astype(BF)
            ga[j, rows] = (u * (s + silu * (1.0 - s))).astype(BF)
            ub[j, rows] = silu.astype(BF)
            return carry

        lax.fori_loop(0, 32, work, 0)

    def hidden_grads(q, first, n):
        def work(i, carry):
            j = (at.z * 2 + first + i // 2) % 16
            rows = pl.ds(pl.multiple_of(64 * q + i % 2 * 32, 32), 32)
            grad = dh_all[j, rows].astype(F32)
            ga[j, rows] = (ga[j, rows].astype(F32) * grad).astype(BF)
            ub[j, rows] = (ub[j, rows].astype(F32) * grad).astype(BF)
            return carry

        lax.fori_loop(0, 2 * n, work, 0)

    def down(lo, n):
        dw[lo : lo + n, :] = rows_dot(flat(hid[:, :, lo : lo + n]), flat(dy_all[...])).astype(BF)

    def wgrad(out, right, lo):
        out[lo : lo + 256, :] = rows_dot(flat(x_all[:, :, lo : lo + 256]), flat(right[...])).astype(BF)

    def back(q, j):
        rows = pl.ds(64 * q, 64)
        return jnp.dot(ga[j, rows], wgt[...], preferred_element_type=F32) + jnp.dot(
            ub[j, rows], wut[...], preferred_element_type=F32
        )

    ways = ((0, at.zp, at.zm), (1, at.zm, at.zp))

    def back_first(q):
        for other in (1, 0):
            value = back(q, at.slab(4, other))
            for way, peer, _ in ways:
                rows = pl.ds(32 * way, 32)
                rstage[q, 0, way, other, rows] = value[32 * way : 32 * way + 32].astype(BF)
                back_sends[q].go(
                    rstage.at[q, 0, way, other, rows],
                    rhalf.at[q, way, other],
                    rring_sem.at[q, 0, way, other],
                    peer,
                )

    def back_step(q, t):
        for other in (1, 0):
            for way, peer, source in ways:
                value = back(q, at.slab((4 - t) * (1 - 2 * way), other))
                out = rstage.at[q, t, way, other]
                if t == 1:
                    back_sends[q].arrived(rhalf.at[q, way, other], rring_sem.at[q, 0, way, other], source)
                    lo = 32 * way
                    out[lo : lo + 32] = (
                        value[lo : lo + 32] + rhalf[q, way, other].astype(F32)
                    ).astype(BF)
                    lo = 32 - lo
                    out[lo : lo + 32] = value[lo : lo + 32].astype(BF)
                else:
                    came = rfull.at[q, t - 2, way, other]
                    back_sends[q].arrived(came, rring_sem.at[q, t - 1, way, other], source)
                    out[...] = (value + came[...].astype(F32)).astype(BF)
                back_sends[q].go(
                    out, rfull.at[q, t - 1, way, other], rring_sem.at[q, t, way, other], peer
                )

    def back_last(q):
        rows = pl.ds(64 * q, 64)
        for other in (1, 0):
            value = back(q, at.slab(0, other))
            for way, _, source in ways:
                came = rfull.at[q, 2, way, other]
                back_sends[q].arrived(came, rring_sem.at[q, 3, way, other], source)
                value = value + came[...].astype(F32)
            if other == 1:
                rpair[q, 0] = value.astype(BF)
                back_sends[q].go(rpair.at[q, 0], rpair.at[q, 1], rring_sem.at[q, 4, 0, 0], at.hp)
            else:
                total[rows] = value + og[rows].astype(F32)

    def back_pair(q):
        rows = pl.ds(64 * q, 64)
        back_sends[q].arrived(rpair.at[q, 1], rring_sem.at[q, 4, 0, 0], at.hp)
        total[rows] = total[rows] + rpair[q, 1].astype(F32)
        gr_out[rows] = total[rows].astype(BF)
        rim_sends.go(
            chunk(gr_out, q), gr_rim.at[1 - q], rim_sem.at[3 - q], at.after if q else at.before
        )

    def fill():
        clear_rim(frame)
        for plane in (0, 1):
            fill_plane(
                frame,
                plane + 1,
                lambda i: px[pl.ds(pl.multiple_of(plane * 64 + i * 16, 16), 16)].astype(F32),
            )

    def mixed(i, value):
        x_all[at.r, pl.ds(pl.multiple_of(i * 16, 16), 16)] = value.astype(BF)

    def tap_store(plane, n, cut, value):
        spot = tap_out.at[n // 2, n % 2 : n % 2 + 1, cut]
        spot[...] = value if plane == 0 else spot[...] + value

    def taps_of(plane):
        tap_totals(total, frame, plane, lambda n, cut, value: tap_store(plane, n, cut, value))
        fill_plane(
            gframe,
            plane + 1,
            lambda i: total[pl.ds(pl.multiple_of(plane * 64 + i * 16, 16), 16)],
        )

    tap_out[13, 1:2] = jnp.zeros((1, tap_out.shape[2]), F32)
    tap_out[14] = jnp.zeros(tap_out.shape[1:], F32)
    tap_out[15] = jnp.zeros(tap_out.shape[1:], F32)
    dy[0].start(chunk(og, 0))
    dy[1].start(chunk(og, 1))
    rim_sends.go(px.at[pl.ds(64, 64)], px_rim.at[0], rim_sem.at[0], at.after)
    rim_sends.go(px.at[pl.ds(0, 64)], px_rim.at[1], rim_sem.at[1], at.before)

    gg[0].start(chunk(gate, 0))
    gg[1].start(chunk(gate, 1))
    ug[1].start(chunk(up, 1))
    ug[0].start(chunk(up, 0))
    fill()
    wgt[...] = wg[...].T
    wut[...] = wu[...].T
    partials(0, [at.r])
    partials(0, dy[0].pair())
    to_mate(0, 0)
    dy_step(0, 1)
    gg[0].pair()
    partials(1, [at.r])
    partials(1, dy[1].pair())
    to_mate(1, 0)
    rims(px_rim, rim_sem, frame)
    convolve(frame, taps, False, lines, mixed)
    gg[1].pair()
    dy_step(0, 2)
    dy_step(1, 1)
    ug[1].pair()
    gg[0].step1()
    gg[1].step1()
    dy_step(0, 3)
    ug[0].pair()
    ug[1].step1()
    gg[0].step2()
    dy_step(1, 2)
    dy_step(0, 4)
    red[0].stage1()
    ug[0].step1()
    dy_step(1, 3)
    ug[1].step2()
    red[0].stage2()
    xg.start(x_all.at[at.r])
    ug[1].step3()
    dy_step(1, 4)
    ug[0].step2()
    gg[1].step2()
    red[1].stage1()
    gg[0].step3()
    red[0].stage3()
    ug[1].rest()
    xg.pair()
    red[1].stage2()
    xg.step(1)
    red[0].stage4()
    hg[0].start()
    red[1].stage3()
    gg[1].step3()
    ug[0].step3()
    ug[0].rest()
    hg[0].pair()
    gg[1].rest()
    swiglu(1)
    red[1].stage4()
    hg[1].start()
    xg.step(2)
    gg[0].rest()
    swiglu(0)
    hg[0].step1()
    hg[1].pair()
    hg[0].step2()
    hg[1].step1()
    xg.step(3)
    hg[0].step3()
    hg[0].rest()
    hidden_grads(0, 8, 2)
    back_first(0)
    hg[1].step2()
    hidden_grads(0, 10, 14)
    back_step(0, 1)
    hg[1].step3()
    hg[1].rest()
    hidden_grads(1, 8, 2)
    back_first(1)
    xg.step(4)
    back_step(0, 2)
    hidden_grads(1, 10, 14)
    back_step(1, 1)
    down(0, 256)
    back_step(0, 3)
    back_step(1, 2)
    wgrad(gw, ga, 0)
    back_last(0)
    back_step(1, 3)
    wgrad(gw, ga, 256)
    back_pair(0)
    back_last(1)
    clear_rim(gframe)
    down(256, 256)
    taps_of(0)
    back_pair(1)
    taps_of(1)
    for n, peer in enumerate(row_peers):
        j = (at.r + n + 1) % 16
        first_taps.go(tap_out.at[j], tap_in.at[at.r], tap_sem.at[0], peer)
    wgrad(uw, ub, 0)
    tap_in[at.r] = tap_out[at.r]
    first_taps.arrived(tap_in.at[pl.ds(0, 15)], tap_sem.at[0], at.hp)
    tap_all[at.r] = jnp.sum(tap_in[...], axis=0)
    for peer in row_peers:
        last_taps.go(tap_all.at[at.r], tap_all.at[at.r], tap_sem.at[1], peer)
    rims(gr_rim, rim_sem.at[pl.ds(2, 2)], gframe)

    def grads(i, value):
        pgrad[pl.ds(pl.multiple_of(i * 16, 16), 16)] = value.astype(BF)

    convolve(gframe, taps, True, lines, grads)
    wgrad(uw, ub, 256)
    down(512, 256)
    down(768, 128)
    last_taps.arrived(tap_all.at[pl.ds(0, 15)], tap_sem.at[1], at.hp)
    for n in range(27):
        e = n % 3
        kgrad[n // 9, n // 3 % 3, e : e + 1, :] = tap_all[n // 2, n % 2 : n % 2 + 1]
    for gather in (*dy, xg, *gg, *ug, *hg, *red):
        gather.finish()
    for q in both:
        sent = x_all.at[pl.ds(0, 15), pl.ds(64 * q, 64)]
        back_sends[q].finish(sent, rring_sem.at[q, 4, 0, 0], at.hp)
    rim_sends.finish(x_all.at[pl.ds(0, 4), pl.ds(0, 64)], rim_sem.at[0], at.hp)
    first_taps.finish(tap_in.at[pl.ds(0, 15)], tap_sem.at[0], at.hp)
    last_taps.finish(tap_in.at[pl.ds(0, 15)], tap_sem.at[1], at.hp)


VM = pl.BlockSpec(memory_space=pltpu.VMEM)


def run(px, og, taps, gate, up, wg, wu, wd):
    feats, units = og.shape[1], gate.shape[1]
    tok, hid = (16, 128, feats), (16, 128, units)
    vm = pltpu.VMEM
    return pl.pallas_call(
        whole,
        out_shape=[
            jax.ShapeDtypeStruct((128, feats), BF),
            jax.ShapeDtypeStruct((3, 3, 3, feats), F32),
            jax.ShapeDtypeStruct((feats, units), BF),
            jax.ShapeDtypeStruct((feats, units), BF),
            jax.ShapeDtypeStruct((units, feats), BF),
        ],
        in_specs=[VM] * 8,
        out_specs=[VM] * 5,
        scratch_shapes=[
            *(vm(s, BF) for s in (tok, tok, hid, hid, hid, hid, hid, hid)),
            vm((feats, units), BF),
            vm((units, feats), BF),
            vm((units, feats), BF),
            vm(hid, BF),
            vm((8, 128, units), BF),
            vm((2, 4, 2, 64, units), BF),
            vm((2, 2, 2, 32, units), BF),
            vm((2, 2, 2, 64, units), BF),
            vm((2, 64, units), BF),
            vm((2, 4, 2, 2, 64, feats), BF),
            vm((2, 2, 2, 32, feats), BF),
            vm((2, 3, 2, 2, 64, feats), BF),
            vm((2, 2, 64, feats), BF),
            vm((2, 64, feats), BF),
            vm((2, 64, feats), BF),
            vm((128, feats), BF),
            vm((3, 4, 10, 8, feats), F32),
            vm((3, 4, 10, 8, feats), F32),
            vm((16, feats), F32),
            vm((128, feats), F32),
            vm((16, 2, feats), F32),
            vm((16, 2, feats), F32),
            vm((16, 2, feats), F32),
            DMA((18,)),
            DMA((2, 17)),
            DMA((17,)),
            DMA((2, 13)),
            DMA((2, 13)),
            DMA((2, 13)),
            DMA((2, 8)),
            DMA((2, 5, 2)),
            DMA((2, 5, 2, 2)),
            DMA((4,)),
            DMA((2,)),
        ],
        compiler_params=pltpu.CompilerParams(
            collective_id=0, has_side_effects=True, vmem_limit_bytes=67043328
        ),
        name="whole",
    )(px, og, taps, gate, up, wg, wu, wd)


def settle(*refs):
    ins, outs, held, (come, go) = refs[:5], refs[5:10], refs[10:15], refs[15:]
    into = [pltpu.make_async_copy(a, v, come.at[i]) for i, (a, v) in enumerate(zip(ins, held))]
    out = [pltpu.make_async_copy(v, b, go.at[i]) for i, (v, b) in enumerate(zip(held, outs))]
    for copy in into:
        copy.start()
    for first, second in zip(into, out):
        first.wait()
        second.start()
    for copy in out:
        copy.wait()


def run_settle(results):
    like = [(a.shape, a.dtype) for a in results]
    return pl.pallas_call(
        settle,
        out_shape=[jax.ShapeDtypeStruct(*a) for a in like],
        in_specs=[pl.BlockSpec(memory_space=pl.ANY)] * 5,
        out_specs=[pl.BlockSpec(memory_space=pl.ANY)] * 5,
        scratch_shapes=[*(pltpu.VMEM(*a) for a in like), DMA((5,)), DMA((5,))],
        name="settle",
    )(*results)


def body(patches, out_grad, conv_kernel, saved_gate, saved_up, w_gate, w_up, w_down):
    planes, height, breadth, features = patches.shape
    own = planes * height * breadth
    results = run(
        patches.reshape(own, features),
        out_grad.reshape(own, features),
        conv_kernel,
        saved_gate,
        saved_up,
        w_gate,
        w_up,
        w_down,
    )
    patch_grad, kernel_grad, gate_wgrad, up_wgrad, down_wgrad = run_settle(results)
    return (
        patch_grad.reshape(patches.shape),
        kernel_grad,
        gate_wgrad,
        up_wgrad,
        down_wgrad,
    )


def solution(mesh):
    return jax.shard_map(
        body,
        mesh=mesh,
        in_specs=(
            P("row", None, None, "col"),
            P("row", None, None, "col"),
            P(None, None, None, "col"),
            P("col", "row"),
            P("col", "row"),
            P("col", "row"),
            P("col", "row"),
            P("row", "col"),
        ),
        out_specs=(
            P("row", None, None, "col"),
            P(None, None, None, "col"),
            P("col", "row"),
            P("col", "row"),
            P("row", "col"),
        ),
        check_vma=False,
    )
```

time: 362 us -> 120 us (0.33)
  waiting for transfers between devices: 224 us -> 0 us
  Pallas kernels: 0 us -> 118 us
  blocking collectives: 46.9 us -> 0 us
  starting transfers between devices: 29.5 us -> 0 us
  matrix products: 28 us -> 0 us
  between operations: 15.1 us -> 0.8 us
  local copies, waits for them, and re-layouts: 10 us -> 0 us
  other arithmetic: 8.01 us -> 0 us
    all_gather x2 -> x0, waiting for transfers between devices: 167 us -> none  [in_one_piece(): lax.all_gather(both, axis, axis=dim, tiled=True)]
    pallas_call x0 -> x2, Pallas kernels: none -> 118 us  [the longest x1 115 us: run(): pl.pallas_call(whole, out_shape=[jax.ShapeDtypeStruct((128, feats), BF),...]
    all_to_all x2 -> x0, waiting for transfers between devices: 52.5 us -> none  [the longest x1 41 us: sum_at_owner(): blocks = lax.all_to_all(in_blocks(x, dim, peers), axis, 0, 0, tiled=True)]
    all_to_all x1 -> x0, blocking collectives: 46.9 us -> none  [sum_at_owner(): blocks = lax.all_to_all(in_blocks(x, dim, peers), axis, 0, 0, tiled=True)]
    dot_general x6 -> x0, matrix products: 28 us -> none  [the longest x1 6.09 us: body(): lax.dot_general(flat_in, gate_grad_all, contract_rows, preferred_element_...]
    all_to_all x2 -> x0, starting transfers between devices: 19.3 us -> none  [the longest x1 9.74 us: from_everyone(): lax.all_to_all(jnp.broadcast_to(x[None], (peers, *x.shape)), axis, 0, 0,...]
    ppermute x4 -> x0, starting transfers between devices: 10.1 us -> none  [the longest x2 7.56 us: padded(): before = lax.ppermute(last, axis, up)]
    ppermute x4 -> x0, waiting for transfers between devices: 4.36 us -> none  [the longest x2 4.36 us: padded(): after = lax.ppermute(first, axis, down)]
  transfers between devices with their start and end apart: 8 -> 0, of which waited for: 5 -> 0; matrix products, arithmetic and copies ran while one was open for 6% -> 0% of each run, Pallas kernels for 0% -> 0%
where the time goes in v3:
time: 120 us; the launch traced here: 119 us
  Pallas kernels  118 us (98%)
    pallas_call x1, Pallas kernels, run(): pl.pallas_call(whole, out_shape=[jax.ShapeDtypeStruct((128, feats), BF),...  115 us
    pallas_call x1, Pallas kernels, run_settle(): pl.pallas_call(settle, out_shape=[jax.ShapeDtypeStruct(*a) for a in like]...  2.91 us

profile of v3, /device:TPU:2, one launch (start us, length us, event | category | flops | bytes accessed | tf_op | source)
XLA Modules:
  0.0 119.0 jit_solution(18161492809857165853)
XLA Ops:
  0.6 115.3 %whole.1 = (bf16[128,512]{1,0:T(8,128)(2,1)}, f32[3,3,3,512]{3,2,1,0:T(4,128)}, bf16[512,896]{1,0:T(8,128)(2,1)}, bf16[512,896]{1,0:T(8,128)(2,1)}, bf16[896,512]{1,0:T(8,128)(2,1)}) custom-call(bf16[128,512]{1,0:T(8,128)(2,1)} %bitcast.3, bf16[128,512]{1,0:T(8,128)(2,1)} %bitcast.4, f32[3,3,3,512]{3,2,1,0:T(4,128)} %taps.1, bf16[128,896]{1,0:T(8,128)(2,1)} %gate.1, ...), custom_call_target="tpu_custom_call" | custom-call | tf_op jit(solution)/shard_map/whole/pallas_call | solution.py:696
  115.9 2.9 %settle.1 = (bf16[128,512]{1,0:T(8,128)(2,1)}, f32[3,3,3,512]{3,2,1,0:T(4,128)}, bf16[512,896]{1,0:T(8,128)(2,1)}, bf16[512,896]{1,0:T(8,128)(2,1)}, bf16[896,512]{1,0:T(8,128)(2,1)}) custom-call(bf16[128,512]{1,0:T(8,128)(2,1)} %get-tuple-element.15.refs_0_, f32[3,3,3,512]{3,2,1,0:T(4,128)} %get-tuple-element.16.refs_1_, ...), custom_call_target="tpu_custom_call" | custom-call | tf_op jit(solution)/shard_map/settle/pallas_call | solution.py:766

commit v4 on v3

--- a/solution.py
+++ b/solution.py
@@ -373,14 +373,13 @@
     mate_sends, back_sends = [stream(), stream()], [stream(), stream()]
     barrier = pltpu.get_barrier_semaphore()
     row_peers = [((at.r + d) % 16, at.c) for d in range(1, 16)]
-    peers = row_peers + [at.xp, at.xm, at.lp, at.kp]
+    peers = [at.zp, at.zm, at.before, at.after, at.xp, at.xm, at.lp, at.kp]
     for peer in peers:
         pl.semaphore_signal(barrier, inc=1, device_id=peer, device_id_type=MESH)
     wdt[...] = wd[...].T
     dy_all[at.r] = og[...]
     g_all[at.c] = gate[...]
     u_all[at.c] = up[...]
-    pl.semaphore_wait(barrier, len(peers))
 
     def reduce(q):
         def put(lo, value):
@@ -555,6 +554,13 @@
     tap_out[13, 1:2] = jnp.zeros((1, tap_out.shape[2]), F32)
     tap_out[14] = jnp.zeros(tap_out.shape[1:], F32)
     tap_out[15] = jnp.zeros(tap_out.shape[1:], F32)
+    wgt[...] = wg[...].T
+    wut[...] = wu[...].T
+    fill()
+    clear_rim(gframe)
+    partials(0, [at.r])
+    partials(1, [at.r])
+    pl.semaphore_wait(barrier, len(peers))
     dy[0].start(chunk(og, 0))
     dy[1].start(chunk(og, 1))
     rim_sends.go(px.at[pl.ds(64, 64)], px_rim.at[0], rim_sem.at[0], at.after)
@@ -564,15 +570,10 @@
     gg[1].start(chunk(gate, 1))
     ug[1].start(chunk(up, 1))
     ug[0].start(chunk(up, 0))
-    fill()
-    wgt[...] = wg[...].T
-    wut[...] = wu[...].T
-    partials(0, [at.r])
     partials(0, dy[0].pair())
     to_mate(0, 0)
     dy_step(0, 1)
     gg[0].pair()
-    partials(1, [at.r])
     partials(1, dy[1].pair())
     to_mate(1, 0)
     rims(px_rim, rim_sem, frame)
@@ -649,7 +650,6 @@
     wgrad(gw, ga, 256)
     back_pair(0)
     back_last(1)
-    clear_rim(gframe)
     down(256, 256)
     taps_of(0)
     back_pair(1)

time: 120 us -> 118 us (0.983)
  Pallas kernels: 118 us -> 116 us
    pallas_call x1, Pallas kernels: 115 us -> 113 us  [run(): pl.pallas_call(whole, out_shape=[jax.ShapeDtypeStruct((128, feats), BF),...]
where the time goes in v4:
time: 118 us; the launch traced here: 117 us
  Pallas kernels  116 us (98%)
    pallas_call x1, Pallas kernels, run(): pl.pallas_call(whole, out_shape=[jax.ShapeDtypeStruct((128, feats), BF),...  113 us
    pallas_call x1, Pallas kernels, run_settle(): pl.pallas_call(settle, out_shape=[jax.ShapeDtypeStruct(*a) for a in like]...  2.91 us

profile of v4, /device:TPU:2, one launch (start us, length us, event | category | flops | bytes accessed | tf_op | source)
XLA Modules:
  0.0 116.9 jit_solution(12931025064599692321)
XLA Ops:
  0.6 113.2 %whole.1 = (bf16[128,512]{1,0:T(8,128)(2,1)}, f32[3,3,3,512]{3,2,1,0:T(4,128)}, bf16[512,896]{1,0:T(8,128)(2,1)}, bf16[512,896]{1,0:T(8,128)(2,1)}, bf16[896,512]{1,0:T(8,128)(2,1)}) custom-call(bf16[128,512]{1,0:T(8,128)(2,1)} %bitcast.3, bf16[128,512]{1,0:T(8,128)(2,1)} %bitcast.4, f32[3,3,3,512]{3,2,1,0:T(4,128)} %taps.1, bf16[128,896]{1,0:T(8,128)(2,1)} %gate.1, ...), custom_call_target="tpu_custom_call" | custom-call | tf_op jit(solution)/shard_map/whole/pallas_call | solution.py:696
  113.8 2.9 %settle.1 = (bf16[128,512]{1,0:T(8,128)(2,1)}, f32[3,3,3,512]{3,2,1,0:T(4,128)}, bf16[512,896]{1,0:T(8,128)(2,1)}, bf16[512,896]{1,0:T(8,128)(2,1)}, bf16[896,512]{1,0:T(8,128)(2,1)}) custom-call(bf16[128,512]{1,0:T(8,128)(2,1)} %get-tuple-element.15.refs_0_, f32[3,3,3,512]{3,2,1,0:T(4,128)} %get-tuple-element.16.refs_1_, ...), custom_call_target="tpu_custom_call" | custom-call | tf_op jit(solution)/shard_map/settle/pallas_call | solution.py:766
